TPU v7x, 1024 devices: a whole 4x8x16 slice. The times are simulated.
1024 devices in a mesh: gx: 16 (over y, core), gy: 4 (over x), gz: 16 (over z).
Axes of the slice: x: 4, y: 8, z: 16, core: 2. Of those that a mesh axis runs over, the one named last changes fastest.
Arguments:
- source: float32 [256, 32, 4096], P('gx', 'gy', 'gz'), may hold values from -8 to 8
- phase_mask: int32 [256, 32, 4096], P('gx', 'gy', 'gz'), may hold values 0 or 1
- density_factor: float32 [256, 32, 4096], P('gx', 'gy', 'gz'), may hold values from 0.5 to 2
Outputs:
- pressure: float32 [256, 32, 4096], P('gx', 'gy', 'gz')
All inputs are finite; a program needn't handle non-finite values. No bound on the sum of `phase_mask` on one device may be relied on, other than what follows from the above.
Results may differ from a plain program's by a relative error of at most 0.0001.
Values sent between devices are 32-bit elements; how exact they have to be, the bound alone decides.
A program may use at most 64 MiB of HBM per device.

v0:
```python
import jax
import jax.numpy as jnp
from jax import lax
from jax.sharding import PartitionSpec as P

LEVELS = 2
COARSE_SWEEPS = 8


GAS_DENSITY = 0.001
RELAXATION = 0.8
NEIGHBOURS = ((1, 0, 0), (-1, 0, 0), (0, 1, 0), (0, -1, 0), (0, 0, 1), (0, 0, -1))


def extended(cells, sides, width):
    for axis, dim in sides:
        count = lax.axis_size(axis)
        ends = count - 1
        head = lax.slice_in_dim(cells, 0, width, axis=dim)
        tail = lax.slice_in_dim(cells, cells.shape[dim] - width, cells.shape[dim], axis=dim)
        cells = jnp.concatenate(
            [
                lax.ppermute(tail, axis, [(i, (i + 1) % count) for i in range(ends)]),
                cells,
                lax.ppermute(head, axis, [((i + 1) % count, i) for i in range(ends)]),
            ],
            axis=dim,
        )
    return cells


def with_halo(x, sides, width):
    edges = {}
    for axis, dim in sides:
        size, length = (lax.axis_size(axis), x.shape[dim])
        up = [(i, (i + 1) % size) for i in range(size - 1)]
        last = lax.slice_in_dim(x, length - width, length, axis=dim)
        initial = lax.slice_in_dim(x, 0, width, axis=dim)
        edges[dim] = (
            lax.ppermute(last, axis, up),
            lax.ppermute(initial, axis, [(b, a) for a, b in up]),
        )
    done = []
    for _, dim in sides:
        low, high = edges[dim]
        around = [(width, width) if d in done else (0, 0) for d in range(x.ndim)]
        x = jnp.concatenate([jnp.pad(low, around), x, jnp.pad(high, around)], axis=dim)
        done.append(dim)
    return x


def shifted(padded, offset):
    return padded[
        1 + offset[0] : padded.shape[0] - 1 + offset[0],
        1 + offset[1] : padded.shape[1] - 1 + offset[1],
        1 + offset[2] : padded.shape[2] - 1 + offset[2],
    ]


def trimmed(cell_values, layers):
    return cell_values[layers:-layers, layers:-layers, layers:-layers]


def coarsen(cell_values):
    return cell_values.reshape(
        cell_values.shape[0] // 2, 2, cell_values.shape[1] // 2, 2, cell_values.shape[2] // 2, 2
    ).sum(axis=(1, 3, 5))


def refine(cell_values):
    widened = jnp.broadcast_to(
        cell_values[:, None, :, None, :, None],
        (cell_values.shape[0], 2, cell_values.shape[1], 2, cell_values.shape[2], 2),
    )
    return widened.reshape(
        2 * cell_values.shape[0], 2 * cell_values.shape[1], 2 * cell_values.shape[2]
    )


def extend(cell_values, layer_count):
    return extended(cell_values, (("gx", 0), ("gy", 1), ("gz", 2)), layer_count)


def face_layer(cell_values):
    return with_halo(cell_values, (("gx", 0), ("gy", 1), ("gz", 2)), 1)


def span_mask(extent, margin, position, devices):
    coords = jnp.arange(extent + 2 * margin, dtype=jnp.int32) - margin + position * extent
    return (coords >= 0) & (coords < extent * devices)


def ownership(cells_shape, margin):
    mask_x = span_mask(cells_shape[0], margin, lax.axis_index("gx"), lax.axis_size("gx"))
    mask_y = span_mask(cells_shape[1], margin, lax.axis_index("gy"), lax.axis_size("gy"))
    mask_z = span_mask(cells_shape[2], margin, lax.axis_index("gz"), lax.axis_size("gz"))
    return mask_x[:, None, None] & mask_y[None, :, None] & mask_z[None, None, :]


def prepare(density_padded, inside):
    centre = shifted(density_padded, (0, 0, 0))
    if inside is not None:
        centre = jnp.where(inside, centre, 1.0)
    couplings = [2.0 / (centre + shifted(density_padded, offset)) for offset in NEIGHBOURS]
    diagonal = couplings[0]
    for coupling in couplings[1:]:
        diagonal = diagonal + coupling
    return (couplings, diagonal)


def operate(padded_values, couplings, diagonal):
    result = diagonal * shifted(padded_values, (0, 0, 0))
    for coupling, offset in zip(couplings, NEIGHBOURS):
        result = result - coupling * shifted(padded_values, offset)
    return result


def coarse_solve(source_here, density):
    couplings, diagonal = prepare(face_layer(density), None)
    iterate = RELAXATION * source_here / diagonal
    for sweep_index in range(COARSE_SWEEPS - 1):
        iterate = (
            iterate
            + RELAXATION
            * (source_here - operate(face_layer(iterate), couplings, diagonal))
            / diagonal
        )
    return iterate


def descend(source_here, densities, prepared, level_index):
    if level_index == LEVELS:
        return coarse_solve(source_here, densities[LEVELS])
    couplings, diagonal, inside = prepared[level_index]
    source_padded = extend(source_here, 2)
    first_sweep = jnp.where(inside, RELAXATION * source_padded / diagonal, 0.0)
    inner_couplings = [trimmed(coupling, 1) for coupling in couplings]
    inner_diagonal = trimmed(diagonal, 1)
    second_sweep = (
        trimmed(first_sweep, 1)
        + RELAXATION
        * (trimmed(source_padded, 1) - operate(first_sweep, inner_couplings, inner_diagonal))
        / inner_diagonal
    )
    second_sweep = jnp.where(trimmed(inside, 1), second_sweep, 0.0)
    core_couplings = [trimmed(coupling, 2) for coupling in couplings]
    core_diagonal = trimmed(diagonal, 2)
    residual = source_here - operate(second_sweep, core_couplings, core_diagonal)
    iterate = trimmed(second_sweep, 1)
    correction = descend(0.5 * coarsen(residual), densities, prepared, level_index + 1)
    iterate = iterate + refine(correction)
    return (
        iterate
        + RELAXATION
        * (source_here - operate(face_layer(iterate), core_couplings, core_diagonal))
        / core_diagonal
    )


def shards(source, phase_mask, density_factor):
    density = jnp.where(phase_mask == 1, GAS_DENSITY, 1.0) * density_factor
    densities = [density]
    for level_index in range(LEVELS):
        densities.append(0.125 * coarsen(densities[-1]))
    prepared = []
    for level_index in range(LEVELS):
        inside = ownership(densities[level_index].shape, 2)
        couplings, diagonal = prepare(extend(densities[level_index], 3), inside)
        prepared.append((couplings, diagonal, inside))
    return descend(source, densities, prepared, 0)


def solution(mesh):
    return jax.shard_map(
        shards,
        mesh=mesh,
        in_specs=(P("gx", "gy", "gz"), P("gx", "gy", "gz"), P("gx", "gy", "gz")),
        out_specs=P("gx", "gy", "gz"),
        check_vma=False,
    )
```

profile of v0, /device:TPU:795, one launch (start us, length us, event | category | flops | bytes accessed | tf_op | source)
XLA Modules:
  0.0 345.6 jit_solution(7320030882750097202)
XLA Ops:
  1.0 5.1 %collective-permute-start.6 = (f32[3,8,256]{2,1,0:T(8,128)S(1)}, f32[3,8,256]{2,1,0:T(8,128)S(1)}, u32[]{:S(2)}, u32[]{:S(2)}) collective-permute-start(f32[3,8,256]{2,1,0:T(8,128)S(1)} %get-tuple-element.42), channel_id=1, source_target_pairs={{0,64},{64,128},{128,192},{192,256},{256,320},{320,384},{384,448},... | collective-permute-start | bytes 73736 | tf_op jit(solution)/shard_map/ppermute | solution.py:23
  6.1 9.8 %reshape.134 = f32[8,2,4,2,128,2]{5,4,3,2,1,0:T(8,128)} reshape(f32[16,8,256]{2,1,0:T(8,128)S(1)} %select_multiply_fusion) | data formatting | bytes 262144 | tf_op jit(solution)/shard_map/reshape | solution.py:65
  15.9 4.0 %reduce_sum.37 = f32[8,4,128]{2,1,0:T(4,128)S(1)} reduce(f32[8,2,4,2,128,2]{5,4,3,2,1,0:T(8,128)} %reshape.134, f32[]{:T(128)} %constant.39.clone.1), dimensions={1,3,5}, to_apply=%region_1.2 | reduce | flops 28672 | bytes 147460 | tf_op jit(solution)/shard_map/reduce_sum | solution.py:67
  21.9 2.4 collective-permute-start.19
  25.5 2.2 collective-permute-start.26
  27.7 3.1 collective-permute-start.27
  33.1 2.5 collective-permute-start.7
  36.2 4.4 %collective-permute-start = (f32[2,8,256]{2,1,0:T(8,128)S(1)}, f32[2,8,256]{2,1,0:T(8,128)S(1)}, u32[]{:S(2)}, u32[]{:S(2)}) collective-permute-start(f32[2,8,256]{2,1,0:T(8,128)S(1)} %get-tuple-element.45), channel_id=1, source_target_pairs={{0,64},{64,128},{128,192},{192,256},{256,320},{320,384},{384,448},... | collective-permute-start | bytes 49160 | tf_op jit(solution)/shard_map/ppermute | solution.py:23
  45.7 4.8 %collective-permute-start.25 = (f32[1,2,64]{2,0,1:T(1,128)}, f32[1,2,64]{2,0,1:T(1,128)S(1)}, u32[]{:S(2)}, u32[]{:S(2)}) collective-permute-start(f32[1,2,64]{2,0,1:T(1,128)} %get-tuple-element.110), channel_id=1, source_target_pairs={{0,64},{64,128},{128,192},{192,256},{256,320},{320,384},{384,448},... | collective-permute-start | bytes 1544 | tf_op jit(solution)/shard_map/ppermute | solution.py:40
  50.5 3.4 collective-permute-start.28
  54.0 3.1 collective-permute-start.2
  57.2 2.2 collective-permute-start.3
  59.4 3.1 collective-permute-start.8
  62.5 2.2 collective-permute-start.9
  64.8 3.1 collective-permute-done.9
  70.0 4.6 %collective-permute-start.11 = (f32[22,14,3]{2,1,0:T(8,128)S(1)}, f32[22,14,3]{2,1,0:T(8,128)S(1)}, u32[]{:S(2)}, u32[]{:S(2)}) collective-permute-start(f32[22,14,3]{2,1,0:T(8,128)S(1)} %get-tuple-element.29), channel_id=1, source_target_pairs={{1,0},{2,1},{3,2},{4,3},{5,4},{6,5},{7,6},{8,7},{9,8},{10,9},{11,1... | collective-permute-start | bytes 11096 | tf_op jit(solution)/shard_map/ppermute | solution.py:25
  74.7 2.8 collective-permute-done.10
  79.4 4.7 %collective-permute-start.5 = (f32[20,12,2]{2,1,0:T(8,128)S(1)}, f32[20,12,2]{2,1,0:T(8,128)S(1)}, u32[]{:S(2)}, u32[]{:S(2)}) collective-permute-start(f32[20,12,2]{2,1,0:T(8,128)S(1)} %get-tuple-element.31), channel_id=1, source_target_pairs={{1,0},{2,1},{3,2},{4,3},{5,4},{6,5},{7,6},{8,7},{9,8},{10,9},{11,1... | collective-permute-start | bytes 5768 | tf_op jit(solution)/shard_map/ppermute | solution.py:25
  85.6 2.4 collective-permute-start.20
  88.0 3.5 %collective-permute-start.21 = (f32[14,3,128]{2,1,0:T(4,128)}, f32[14,3,128]{2,1,0:T(4,128)}, u32[]{:S(2)}, u32[]{:S(2)}) collective-permute-start(f32[14,3,128]{2,1,0:T(4,128)} %get-tuple-element.51), channel_id=1, source_target_pairs={{16,0},{32,16},{48,32},{17,1},{33,17},{49,33},{18,2},{34,18},{50,3... | collective-permute-start | bytes 64520 | tf_op jit(solution)/shard_map/ppermute | solution.py:25
  95.3 9.8 %reshape.133 = f32[8,2,4,2,128,2]{5,4,3,2,1,0:T(8,128)} reshape(f32[16,8,256]{2,1,0:T(8,128)S(1)} %fusion.36) | data formatting | bytes 262144 | tf_op jit(solution)/shard_map/reshape | solution.py:65
  105.0 4.1 %reduce_sum.36 = f32[8,4,128]{2,1,0:T(4,128)S(1)} reduce(f32[8,2,4,2,128,2]{5,4,3,2,1,0:T(8,128)} %reshape.133, f32[]{:T(128)} %constant.39.clone.1), dimensions={1,3,5}, to_apply=%region_0.1 | reduce | flops 28672 | bytes 147460 | tf_op jit(solution)/shard_map/reduce_sum | solution.py:67
  109.1 4.6 %collective-permute-start.12 = (f32[2,4,128]{2,1,0:T(4,128)S(1)}, f32[2,4,128]{2,1,0:T(4,128)S(1)}, u32[]{:S(2)}, u32[]{:S(2)}) collective-permute-start(f32[2,4,128]{2,1,0:T(4,128)S(1)} %get-tuple-element.62), channel_id=1, source_target_pairs={{0,64},{64,128},{128,192},{192,256},{256,320},{320,384},{384,448},... | collective-permute-start | bytes 12296 | tf_op jit(solution)/shard_map/ppermute | solution.py:23
  116.5 3.4 collective-permute-done.13
  121.8 3.4 collective-permute-start.15
  127.2 4.6 %collective-permute-start.23 = (f32[14,10,3]{2,1,0:T(8,128)S(1)}, f32[14,10,3]{2,1,0:T(8,128)S(1)}, u32[]{:S(2)}, u32[]{:S(2)}) collective-permute-start(f32[14,10,3]{2,1,0:T(8,128)S(1)} %get-tuple-element.47), channel_id=1, source_target_pairs={{1,0},{2,1},{3,2},{4,3},{5,4},{6,5},{7,6},{8,7},{9,8},{10,9},{11,1... | collective-permute-start | bytes 5048 | tf_op jit(solution)/shard_map/ppermute | solution.py:25
  134.5 4.9 %collective-permute-start.17 = (f32[12,8,2]{2,1,0:T(8,128)S(1)}, f32[12,8,2]{2,1,0:T(8,128)S(1)}, u32[]{:S(2)}, u32[]{:S(2)}) collective-permute-start(f32[12,8,2]{2,1,0:T(8,128)S(1)} %get-tuple-element.49), channel_id=1, source_target_pairs={{1,0},{2,1},{3,2},{4,3},{5,4},{6,5},{7,6},{8,7},{9,8},{10,9},{11,1... | collective-permute-start | bytes 2312 | tf_op jit(solution)/shard_map/ppermute | solution.py:25
  149.7 3.4 collective-permute-start.33
  153.0 3.5 %collective-permute-start.30 = (f32[1,2,64]{2,0,1:T(1,128)S(1)}, f32[1,2,64]{2,0,1:T(1,128)S(1)}, u32[]{:S(2)}, u32[]{:S(2)}) collective-permute-start(f32[1,2,64]{2,0,1:T(1,128)S(1)} %get-tuple-element.103), channel_id=1, source_target_pairs={{64,0},{128,64},{192,128},{256,192},{320,256},{384,320},{448,384},... | collective-permute-start | bytes 1544 | tf_op jit(solution)/shard_map/ppermute | solution.py:41
  156.6 3.2 collective-permute-start.31
  159.8 4.6 %collective-permute-start.34 = (f32[4,2,1]{2,0,1:T(4,128)S(1)}, f32[4,2,1]{2,0,1:T(4,128)S(1)}, u32[]{:S(2)}, u32[]{:S(2)}) collective-permute-start(f32[4,2,1]{2,0,1:T(4,128)S(1)} %get-tuple-element.100), channel_id=1, source_target_pairs={{1,0},{2,1},{3,2},{4,3},{5,4},{6,5},{7,6},{8,7},{9,8},{10,9},{11,1... | collective-permute-start | bytes 104 | tf_op jit(solution)/shard_map/ppermute | solution.py:41
  166.4 3.6 %collective-permute-done.35 = f32[4,2,1]{2,0,1:T(4,128)S(1)} collective-permute-done((f32[4,2,1]{2,0,1:T(4,128)S(1)}, f32[4,2,1]{2,0,1:T(4,128)S(1)}, u32[]{:S(2)}, u32[]{:S(2)}) %collective-permute-start.35) | collective-permute-done | bytes 64 | tf_op jit(solution)/shard_map/ppermute | solution.py:40
  172.1 3.4 collective-permute-start.39
  175.5 2.8 collective-permute-start.36
  178.3 4.0 %collective-permute-start.37 = (f32[1,2,64]{2,0,1:T(1,128)S(1)}, f32[1,2,64]{2,0,1:T(1,128)S(1)}, u32[]{:S(2)}, u32[]{:S(2)}) collective-permute-start(f32[1,2,64]{2,0,1:T(1,128)S(1)} %get-tuple-element.96), channel_id=1, source_target_pairs={{0,64},{64,128},{128,192},{192,256},{256,320},{320,384},{384,448},... | collective-permute-start | bytes 1544 | tf_op jit(solution)/shard_map/ppermute | solution.py:40
  184.2 3.4 collective-permute-start.41
  187.6 2.1 collective-permute-done.41
  191.9 3.4 collective-permute-start.45
  197.3 4.7 %collective-permute-start.43 = (f32[1,2,64]{2,0,1:T(1,128)S(1)}, f32[1,2,64]{2,0,1:T(1,128)S(1)}, u32[]{:S(2)}, u32[]{:S(2)}) collective-permute-start(f32[1,2,64]{2,0,1:T(1,128)S(1)} %get-tuple-element.90), channel_id=1, source_target_pairs={{0,64},{64,128},{128,192},{192,256},{256,320},{320,384},{384,448},... | collective-permute-start | bytes 1544 | tf_op jit(solution)/shard_map/ppermute | solution.py:40
  204.0 3.4 collective-permute-start.47
  207.4 2.1 collective-permute-done.47
  211.6 3.4 collective-permute-start.51
  216.9 4.9 %collective-permute-start.49 = (f32[1,2,64]{2,0,1:T(1,128)S(1)}, f32[1,2,64]{2,0,1:T(1,128)S(1)}, u32[]{:S(2)}, u32[]{:S(2)}) collective-permute-start(f32[1,2,64]{2,0,1:T(1,128)S(1)} %get-tuple-element.84), channel_id=1, source_target_pairs={{0,64},{64,128},{128,192},{192,256},{256,320},{320,384},{384,448},... | collective-permute-start | bytes 1544 | tf_op jit(solution)/shard_map/ppermute | solution.py:40
  223.7 3.4 collective-permute-start.53
  231.4 3.4 collective-permute-start.57
  236.7 4.9 %collective-permute-start.55 = (f32[1,2,64]{2,0,1:T(1,128)S(1)}, f32[1,2,64]{2,0,1:T(1,128)S(1)}, u32[]{:S(2)}, u32[]{:S(2)}) collective-permute-start(f32[1,2,64]{2,0,1:T(1,128)S(1)} %get-tuple-element.78), channel_id=1, source_target_pairs={{0,64},{64,128},{128,192},{192,256},{256,320},{320,384},{384,448},... | collective-permute-start | bytes 1544 | tf_op jit(solution)/shard_map/ppermute | solution.py:40
  243.5 3.4 collective-permute-start.59
  251.2 3.4 collective-permute-start.63
  256.5 4.9 %collective-permute-start.61 = (f32[1,2,64]{2,0,1:T(1,128)S(1)}, f32[1,2,64]{2,0,1:T(1,128)S(1)}, u32[]{:S(2)}, u32[]{:S(2)}) collective-permute-start(f32[1,2,64]{2,0,1:T(1,128)S(1)} %get-tuple-element.72), channel_id=1, source_target_pairs={{0,64},{64,128},{128,192},{192,256},{256,320},{320,384},{384,448},... | collective-permute-start | bytes 1544 | tf_op jit(solution)/shard_map/ppermute | solution.py:40
  263.3 3.4 collective-permute-start.65
  270.9 3.4 collective-permute-start.69
  276.3 4.9 %collective-permute-start.67 = (f32[1,2,64]{2,0,1:T(1,128)S(1)}, f32[1,2,64]{2,0,1:T(1,128)S(1)}, u32[]{:S(2)}, u32[]{:S(2)}) collective-permute-start(f32[1,2,64]{2,0,1:T(1,128)S(1)} %get-tuple-element.66), channel_id=1, source_target_pairs={{0,64},{64,128},{128,192},{192,256},{256,320},{320,384},{384,448},... | collective-permute-start | bytes 1544 | tf_op jit(solution)/shard_map/ppermute | solution.py:40
  283.1 3.4 collective-permute-start.71
  292.7 3.4 collective-permute-start.75
  298.0 4.9 %collective-permute-start.73 = (f32[1,4,128]{2,1,0:T(4,128)S(1)}, f32[1,4,128]{2,1,0:T(4,128)S(1)}, u32[]{:S(2)}, u32[]{:S(2)}) collective-permute-start(f32[1,4,128]{2,1,0:T(4,128)S(1)} %get-tuple-element.56), channel_id=1, source_target_pairs={{0,64},{64,128},{128,192},{192,256},{256,320},{320,384},{384,448},... | collective-permute-start | bytes 6152 | tf_op jit(solution)/shard_map/ppermute | solution.py:40
  304.9 3.4 collective-permute-start.77
  308.3 2.3 collective-permute-done.77
  311.8 3.9 %broadcast_in_dim.57 = f32[8,2,4,2,128,2]{5,4,3,2,1,0:T(8,128)} broadcast(f32[8,4,128]{2,1,0:T(4,128)S(1)} %fusion.65), dimensions={0,2,4} | broadcast | bytes 147456 | tf_op jit(solution)/shard_map/broadcast_in_dim | solution.py:71
  315.8 6.9 %reshape.137 = f32[16,8,256]{2,1,0:T(8,128)S(1)} reshape(f32[8,2,4,2,128,2]{5,4,3,2,1,0:T(8,128)} %broadcast_in_dim.57) | data formatting | bytes 262144 | tf_op jit(solution)/shard_map/reshape | solution.py:75
  324.8 3.4 collective-permute-start.81
  330.1 4.9 %collective-permute-start.79 = (f32[1,8,256]{2,1,0:T(8,128)S(1)}, f32[1,8,256]{2,1,0:T(8,128)S(1)}, u32[]{:S(2)}, u32[]{:S(2)}) collective-permute-start(f32[1,8,256]{2,1,0:T(8,128)S(1)} %get-tuple-element.38), channel_id=1, source_target_pairs={{0,64},{64,128},{128,192},{192,256},{256,320},{320,384},{384,448},... | collective-permute-start | bytes 24584 | tf_op jit(solution)/shard_map/ppermute | solution.py:40
  337.0 3.4 collective-permute-start.83
  340.4 2.8 collective-permute-done.83
  343.2 2.4 fusion.23
  (266 shorter events, 100.7 us)
Async XLA Ops:
  1.0 53.0 %collective-permute-start.6 = (f32[3,8,256]{2,1,0:T(8,128)S(1)}, f32[3,8,256]{2,1,0:T(8,128)S(1)}, u32[]{:S(2)}, u32[]{:S(2)}) collective-permute-start(f32[3,8,256]{2,1,0:T(8,128)S(1)} %get-tuple-element.42), channel_id=1, source_target_pairs={{0,64},{64,128},{128,192},{192,256},{256,320},{320,384},{384,448},... | collective-permute-start | bytes 73736 | tf_op jit(solution)/shard_map/ppermute | solution.py:23
  19.9 21.2 %collective-permute-start.18 = (f32[3,4,128]{2,1,0:T(4,128)S(1)}, f32[3,4,128]{2,1,0:T(4,128)S(1)}, u32[]{:S(2)}, u32[]{:S(2)}) collective-permute-start(f32[3,4,128]{2,1,0:T(4,128)S(1)} %get-tuple-element.60), channel_id=1, source_target_pairs={{0,64},{64,128},{128,192},{192,256},{256,320},{320,384},{384,448},... | collective-permute-start | bytes 18440 | tf_op jit(solution)/shard_map/ppermute | solution.py:23
  21.9 21.2 %collective-permute-start.19 = (f32[3,4,128]{2,1,0:T(4,128)S(1)}, f32[3,4,128]{2,1,0:T(4,128)S(1)}, u32[]{:S(2)}, u32[]{:S(2)}) collective-permute-start(f32[3,4,128]{2,1,0:T(4,128)S(1)} %get-tuple-element.61), channel_id=1, source_target_pairs={{64,0},{128,64},{192,128},{256,192},{320,256},{384,320},{448,384},... | collective-permute-start | bytes 18440 | tf_op jit(solution)/shard_map/ppermute | solution.py:25
  25.5 7.6 %collective-permute-start.26 = (f32[4,1,64]{2,0,1:T(4,128)S(1)}, f32[4,1,64]{2,0,1:T(4,128)S(1)}, u32[]{:S(2)}, u32[]{:S(2)}) collective-permute-start(f32[4,1,64]{2,0,1:T(4,128)S(1)} %get-tuple-element.109), channel_id=1, source_target_pairs={{16,0},{32,16},{48,32},{17,1},{33,17},{49,33},{18,2},{34,18},{50,3... | collective-permute-start | bytes 3080 | tf_op jit(solution)/shard_map/ppermute | solution.py:41
  27.7 8.5 %collective-permute-start.27 = (f32[4,1,64]{2,0,1:T(4,128)S(1)}, f32[4,1,64]{2,0,1:T(4,128)S(1)}, u32[]{:S(2)}, u32[]{:S(2)}) collective-permute-start(f32[4,1,64]{2,0,1:T(4,128)S(1)} %get-tuple-element.108), channel_id=1, source_target_pairs={{0,16},{16,32},{32,48},{1,17},{17,33},{33,49},{2,18},{18,34},{34,5... | collective-permute-start | bytes 3080 | tf_op jit(solution)/shard_map/ppermute | solution.py:40
  33.1 24.1 %collective-permute-start.7 = (f32[3,8,256]{2,1,0:T(8,128)S(1)}, f32[3,8,256]{2,1,0:T(8,128)S(1)}, u32[]{:S(2)}, u32[]{:S(2)}) collective-permute-start(f32[3,8,256]{2,1,0:T(8,128)S(1)} %get-tuple-element.43), channel_id=1, source_target_pairs={{64,0},{128,64},{192,128},{256,192},{320,256},{384,320},{448,384},... | collective-permute-start | bytes 73736 | tf_op jit(solution)/shard_map/ppermute | solution.py:25
  36.2 9.5 %collective-permute-start = (f32[2,8,256]{2,1,0:T(8,128)S(1)}, f32[2,8,256]{2,1,0:T(8,128)S(1)}, u32[]{:S(2)}, u32[]{:S(2)}) collective-permute-start(f32[2,8,256]{2,1,0:T(8,128)S(1)} %get-tuple-element.45), channel_id=1, source_target_pairs={{0,64},{64,128},{128,192},{192,256},{256,320},{320,384},{384,448},... | collective-permute-start | bytes 49160 | tf_op jit(solution)/shard_map/ppermute | solution.py:23
  41.1 9.4 %collective-permute-start.1 = (f32[2,8,256]{2,1,0:T(8,128)S(1)}, f32[2,8,256]{2,1,0:T(8,128)S(1)}, u32[]{:S(2)}, u32[]{:S(2)}) collective-permute-start(f32[2,8,256]{2,1,0:T(8,128)S(1)} %get-tuple-element.44), channel_id=1, source_target_pairs={{64,0},{128,64},{192,128},{256,192},{320,256},{384,320},{448,384},... | collective-permute-start | bytes 49160 | tf_op jit(solution)/shard_map/ppermute | solution.py:25
  43.1 103.8 %collective-permute-start.24 = (f32[1,2,64]{2,0,1:T(1,128)}, f32[1,2,64]{2,0,1:T(1,128)S(1)}, u32[]{:S(2)}, u32[]{:S(2)}) collective-permute-start(f32[1,2,64]{2,0,1:T(1,128)} %get-tuple-element.111), channel_id=1, source_target_pairs={{64,0},{128,64},{192,128},{256,192},{320,256},{384,320},{448,384},... | collective-permute-start | bytes 1544 | tf_op jit(solution)/shard_map/ppermute | solution.py:41
  45.7 101.2 %collective-permute-start.25 = (f32[1,2,64]{2,0,1:T(1,128)}, f32[1,2,64]{2,0,1:T(1,128)S(1)}, u32[]{:S(2)}, u32[]{:S(2)}) collective-permute-start(f32[1,2,64]{2,0,1:T(1,128)} %get-tuple-element.110), channel_id=1, source_target_pairs={{0,64},{64,128},{128,192},{192,256},{256,320},{320,384},{384,448},... | collective-permute-start | bytes 1544 | tf_op jit(solution)/shard_map/ppermute | solution.py:40
  50.5 96.3 %collective-permute-start.28 = (f32[4,2,1]{2,0,1:T(4,128)}, f32[4,2,1]{2,0,1:T(4,128)}, u32[]{:S(2)}, u32[]{:S(2)}) collective-permute-start(f32[4,2,1]{2,0,1:T(4,128)} %get-tuple-element.107), channel_id=1, source_target_pairs={{1,0},{2,1},{3,2},{4,3},{5,4},{6,5},{7,6},{8,7},{9,8},{10,9},{11,1... | collective-permute-start | bytes 104 | tf_op jit(solution)/shard_map/ppermute | solution.py:41
  68.1 9.4 %collective-permute-start.10 = (f32[22,14,3]{2,1,0:T(8,128)S(1)}, f32[22,14,3]{2,1,0:T(8,128)S(1)}, u32[]{:S(2)}, u32[]{:S(2)}) collective-permute-start(f32[22,14,3]{2,1,0:T(8,128)S(1)} %get-tuple-element.28), channel_id=1, source_target_pairs={{0,1},{1,2},{2,3},{3,4},{4,5},{5,6},{6,7},{7,8},{8,9},{9,10},{10,1... | collective-permute-start | bytes 11096 | tf_op jit(solution)/shard_map/ppermute | solution.py:23
  70.0 9.4 %collective-permute-start.11 = (f32[22,14,3]{2,1,0:T(8,128)S(1)}, f32[22,14,3]{2,1,0:T(8,128)S(1)}, u32[]{:S(2)}, u32[]{:S(2)}) collective-permute-start(f32[22,14,3]{2,1,0:T(8,128)S(1)} %get-tuple-element.29), channel_id=1, source_target_pairs={{1,0},{2,1},{3,2},{4,3},{5,4},{6,5},{7,6},{8,7},{9,8},{10,9},{11,1... | collective-permute-start | bytes 11096 | tf_op jit(solution)/shard_map/ppermute | solution.py:25
  77.5 8.2 %collective-permute-start.4 = (f32[20,12,2]{2,1,0:T(8,128)S(1)}, f32[20,12,2]{2,1,0:T(8,128)S(1)}, u32[]{:S(2)}, u32[]{:S(2)}) collective-permute-start(f32[20,12,2]{2,1,0:T(8,128)S(1)} %get-tuple-element.30), channel_id=1, source_target_pairs={{0,1},{1,2},{2,3},{3,4},{4,5},{5,6},{6,7},{7,8},{8,9},{9,10},{10,1... | collective-permute-start | bytes 5768 | tf_op jit(solution)/shard_map/ppermute | solution.py:23
  79.4 8.6 %collective-permute-start.5 = (f32[20,12,2]{2,1,0:T(8,128)S(1)}, f32[20,12,2]{2,1,0:T(8,128)S(1)}, u32[]{:S(2)}, u32[]{:S(2)}) collective-permute-start(f32[20,12,2]{2,1,0:T(8,128)S(1)} %get-tuple-element.31), channel_id=1, source_target_pairs={{1,0},{2,1},{3,2},{4,3},{5,4},{6,5},{7,6},{8,7},{9,8},{10,9},{11,1... | collective-permute-start | bytes 5768 | tf_op jit(solution)/shard_map/ppermute | solution.py:25
  85.6 23.5 %collective-permute-start.20 = (f32[14,3,128]{2,1,0:T(4,128)}, f32[14,3,128]{2,1,0:T(4,128)}, u32[]{:S(2)}, u32[]{:S(2)}) collective-permute-start(f32[14,3,128]{2,1,0:T(4,128)} %get-tuple-element.50), channel_id=1, source_target_pairs={{0,16},{16,32},{32,48},{1,17},{17,33},{33,49},{2,18},{18,34},{34,5... | collective-permute-start | bytes 64520 | tf_op jit(solution)/shard_map/ppermute | solution.py:23
  88.0 25.7 %collective-permute-start.21 = (f32[14,3,128]{2,1,0:T(4,128)}, f32[14,3,128]{2,1,0:T(4,128)}, u32[]{:S(2)}, u32[]{:S(2)}) collective-permute-start(f32[14,3,128]{2,1,0:T(4,128)} %get-tuple-element.51), channel_id=1, source_target_pairs={{16,0},{32,16},{48,32},{17,1},{33,17},{49,33},{18,2},{34,18},{50,3... | collective-permute-start | bytes 64520 | tf_op jit(solution)/shard_map/ppermute | solution.py:25
  109.1 7.4 %collective-permute-start.12 = (f32[2,4,128]{2,1,0:T(4,128)S(1)}, f32[2,4,128]{2,1,0:T(4,128)S(1)}, u32[]{:S(2)}, u32[]{:S(2)}) collective-permute-start(f32[2,4,128]{2,1,0:T(4,128)S(1)} %get-tuple-element.62), channel_id=1, source_target_pairs={{0,64},{64,128},{128,192},{192,256},{256,320},{320,384},{384,448},... | collective-permute-start | bytes 12296 | tf_op jit(solution)/shard_map/ppermute | solution.py:23
  113.7 6.1 %collective-permute-start.13 = (f32[2,4,128]{2,1,0:T(4,128)S(1)}, f32[2,4,128]{2,1,0:T(4,128)S(1)}, u32[]{:S(2)}, u32[]{:S(2)}) collective-permute-start(f32[2,4,128]{2,1,0:T(4,128)S(1)} %get-tuple-element.63), channel_id=1, source_target_pairs={{64,0},{128,64},{192,128},{256,192},{320,256},{384,320},{448,384},... | collective-permute-start | bytes 12296 | tf_op jit(solution)/shard_map/ppermute | solution.py:25
  125.3 7.2 %collective-permute-start.22 = (f32[14,10,3]{2,1,0:T(8,128)S(1)}, f32[14,10,3]{2,1,0:T(8,128)S(1)}, u32[]{:S(2)}, u32[]{:S(2)}) collective-permute-start(f32[14,10,3]{2,1,0:T(8,128)S(1)} %get-tuple-element.46), channel_id=1, source_target_pairs={{0,1},{1,2},{2,3},{3,4},{4,5},{5,6},{6,7},{7,8},{8,9},{9,10},{10,1... | collective-permute-start | bytes 5048 | tf_op jit(solution)/shard_map/ppermute | solution.py:23
  127.2 7.2 %collective-permute-start.23 = (f32[14,10,3]{2,1,0:T(8,128)S(1)}, f32[14,10,3]{2,1,0:T(8,128)S(1)}, u32[]{:S(2)}, u32[]{:S(2)}) collective-permute-start(f32[14,10,3]{2,1,0:T(8,128)S(1)} %get-tuple-element.47), channel_id=1, source_target_pairs={{1,0},{2,1},{3,2},{4,3},{5,4},{6,5},{7,6},{8,7},{9,8},{10,9},{11,1... | collective-permute-start | bytes 5048 | tf_op jit(solution)/shard_map/ppermute | solution.py:25
  132.6 7.8 %collective-permute-start.16 = (f32[12,8,2]{2,1,0:T(8,128)S(1)}, f32[12,8,2]{2,1,0:T(8,128)S(1)}, u32[]{:S(2)}, u32[]{:S(2)}) collective-permute-start(f32[12,8,2]{2,1,0:T(8,128)S(1)} %get-tuple-element.48), channel_id=1, source_target_pairs={{0,1},{1,2},{2,3},{3,4},{4,5},{5,6},{6,7},{7,8},{8,9},{9,10},{10,1... | collective-permute-start | bytes 2312 | tf_op jit(solution)/shard_map/ppermute | solution.py:23
  134.5 8.0 %collective-permute-start.17 = (f32[12,8,2]{2,1,0:T(8,128)S(1)}, f32[12,8,2]{2,1,0:T(8,128)S(1)}, u32[]{:S(2)}, u32[]{:S(2)}) collective-permute-start(f32[12,8,2]{2,1,0:T(8,128)S(1)} %get-tuple-element.49), channel_id=1, source_target_pairs={{1,0},{2,1},{3,2},{4,3},{5,4},{6,5},{7,6},{8,7},{9,8},{10,9},{11,1... | collective-permute-start | bytes 2312 | tf_op jit(solution)/shard_map/ppermute | solution.py:25
  140.4 6.5 %collective-permute-start.29 = (f32[4,2,1]{2,0,1:T(4,128)}, f32[4,2,1]{2,0,1:T(4,128)}, u32[]{:S(2)}, u32[]{:S(2)}) collective-permute-start(f32[4,2,1]{2,0,1:T(4,128)} %get-tuple-element.106), channel_id=1, source_target_pairs={{0,1},{1,2},{2,3},{3,4},{4,5},{5,6},{6,7},{7,8},{8,9},{9,10},{10,1... | collective-permute-start | bytes 104 | tf_op jit(solution)/shard_map/ppermute | solution.py:40
  147.7 16.7 %collective-permute-start.32 = (f32[4,1,64]{2,0,1:T(4,128)S(1)}, f32[4,1,64]{2,0,1:T(4,128)S(1)}, u32[]{:S(2)}, u32[]{:S(2)}) collective-permute-start(f32[4,1,64]{2,0,1:T(4,128)S(1)} %get-tuple-element.105), channel_id=1, source_target_pairs={{16,0},{32,16},{48,32},{17,1},{33,17},{49,33},{18,2},{34,18},{50,3... | collective-permute-start | bytes 3080 | tf_op jit(solution)/shard_map/ppermute | solution.py:41
  149.7 16.7 %collective-permute-start.33 = (f32[4,1,64]{2,0,1:T(4,128)S(1)}, f32[4,1,64]{2,0,1:T(4,128)S(1)}, u32[]{:S(2)}, u32[]{:S(2)}) collective-permute-start(f32[4,1,64]{2,0,1:T(4,128)S(1)} %get-tuple-element.104), channel_id=1, source_target_pairs={{0,16},{16,32},{32,48},{1,17},{17,33},{33,49},{2,18},{18,34},{34,5... | collective-permute-start | bytes 3080 | tf_op jit(solution)/shard_map/ppermute | solution.py:40
  153.0 16.9 %collective-permute-start.30 = (f32[1,2,64]{2,0,1:T(1,128)S(1)}, f32[1,2,64]{2,0,1:T(1,128)S(1)}, u32[]{:S(2)}, u32[]{:S(2)}) collective-permute-start(f32[1,2,64]{2,0,1:T(1,128)S(1)} %get-tuple-element.103), channel_id=1, source_target_pairs={{64,0},{128,64},{192,128},{256,192},{320,256},{384,320},{448,384},... | collective-permute-start | bytes 1544 | tf_op jit(solution)/shard_map/ppermute | solution.py:41
  156.6 13.4 %collective-permute-start.31 = (f32[1,2,64]{2,0,1:T(1,128)S(1)}, f32[1,2,64]{2,0,1:T(1,128)S(1)}, u32[]{:S(2)}, u32[]{:S(2)}) collective-permute-start(f32[1,2,64]{2,0,1:T(1,128)S(1)} %get-tuple-element.102), channel_id=1, source_target_pairs={{0,64},{64,128},{128,192},{192,256},{256,320},{320,384},{384,448},... | collective-permute-start | bytes 1544 | tf_op jit(solution)/shard_map/ppermute | solution.py:40
  159.8 6.6 %collective-permute-start.34 = (f32[4,2,1]{2,0,1:T(4,128)S(1)}, f32[4,2,1]{2,0,1:T(4,128)S(1)}, u32[]{:S(2)}, u32[]{:S(2)}) collective-permute-start(f32[4,2,1]{2,0,1:T(4,128)S(1)} %get-tuple-element.100), channel_id=1, source_target_pairs={{1,0},{2,1},{3,2},{4,3},{5,4},{6,5},{7,6},{8,7},{9,8},{10,9},{11,1... | collective-permute-start | bytes 104 | tf_op jit(solution)/shard_map/ppermute | solution.py:41
  170.2 14.0 %collective-permute-start.38 = (f32[4,1,64]{2,0,1:T(4,128)S(1)}, f32[4,1,64]{2,0,1:T(4,128)S(1)}, u32[]{:S(2)}, u32[]{:S(2)}) collective-permute-start(f32[4,1,64]{2,0,1:T(4,128)S(1)} %get-tuple-element.99), channel_id=1, source_target_pairs={{16,0},{32,16},{48,32},{17,1},{33,17},{49,33},{18,2},{34,18},{50,3... | collective-permute-start | bytes 3080 | tf_op jit(solution)/shard_map/ppermute | solution.py:41
  172.1 15.5 %collective-permute-start.39 = (f32[4,1,64]{2,0,1:T(4,128)S(1)}, f32[4,1,64]{2,0,1:T(4,128)S(1)}, u32[]{:S(2)}, u32[]{:S(2)}) collective-permute-start(f32[4,1,64]{2,0,1:T(4,128)S(1)} %get-tuple-element.98), channel_id=1, source_target_pairs={{0,16},{16,32},{32,48},{1,17},{17,33},{33,49},{2,18},{18,34},{34,5... | collective-permute-start | bytes 3080 | tf_op jit(solution)/shard_map/ppermute | solution.py:40
  175.5 14.3 %collective-permute-start.36 = (f32[1,2,64]{2,0,1:T(1,128)S(1)}, f32[1,2,64]{2,0,1:T(1,128)S(1)}, u32[]{:S(2)}, u32[]{:S(2)}) collective-permute-start(f32[1,2,64]{2,0,1:T(1,128)S(1)} %get-tuple-element.97), channel_id=1, source_target_pairs={{64,0},{128,64},{192,128},{256,192},{320,256},{384,320},{448,384},... | collective-permute-start | bytes 1544 | tf_op jit(solution)/shard_map/ppermute | solution.py:41
  178.3 11.5 %collective-permute-start.37 = (f32[1,2,64]{2,0,1:T(1,128)S(1)}, f32[1,2,64]{2,0,1:T(1,128)S(1)}, u32[]{:S(2)}, u32[]{:S(2)}) collective-permute-start(f32[1,2,64]{2,0,1:T(1,128)S(1)} %get-tuple-element.96), channel_id=1, source_target_pairs={{0,64},{64,128},{128,192},{192,256},{256,320},{320,384},{384,448},... | collective-permute-start | bytes 1544 | tf_op jit(solution)/shard_map/ppermute | solution.py:40
  189.9 14.0 %collective-permute-start.44 = (f32[4,1,64]{2,0,1:T(4,128)S(1)}, f32[4,1,64]{2,0,1:T(4,128)S(1)}, u32[]{:S(2)}, u32[]{:S(2)}) collective-permute-start(f32[4,1,64]{2,0,1:T(4,128)S(1)} %get-tuple-element.93), channel_id=1, source_target_pairs={{16,0},{32,16},{48,32},{17,1},{33,17},{49,33},{18,2},{34,18},{50,3... | collective-permute-start | bytes 3080 | tf_op jit(solution)/shard_map/ppermute | solution.py:41
  191.9 15.5 %collective-permute-start.45 = (f32[4,1,64]{2,0,1:T(4,128)S(1)}, f32[4,1,64]{2,0,1:T(4,128)S(1)}, u32[]{:S(2)}, u32[]{:S(2)}) collective-permute-start(f32[4,1,64]{2,0,1:T(4,128)S(1)} %get-tuple-element.92), channel_id=1, source_target_pairs={{0,16},{16,32},{32,48},{1,17},{17,33},{33,49},{2,18},{18,34},{34,5... | collective-permute-start | bytes 3080 | tf_op jit(solution)/shard_map/ppermute | solution.py:40
  195.2 14.3 %collective-permute-start.42 = (f32[1,2,64]{2,0,1:T(1,128)S(1)}, f32[1,2,64]{2,0,1:T(1,128)S(1)}, u32[]{:S(2)}, u32[]{:S(2)}) collective-permute-start(f32[1,2,64]{2,0,1:T(1,128)S(1)} %get-tuple-element.91), channel_id=1, source_target_pairs={{64,0},{128,64},{192,128},{256,192},{320,256},{384,320},{448,384},... | collective-permute-start | bytes 1544 | tf_op jit(solution)/shard_map/ppermute | solution.py:41
  197.3 12.2 %collective-permute-start.43 = (f32[1,2,64]{2,0,1:T(1,128)S(1)}, f32[1,2,64]{2,0,1:T(1,128)S(1)}, u32[]{:S(2)}, u32[]{:S(2)}) collective-permute-start(f32[1,2,64]{2,0,1:T(1,128)S(1)} %get-tuple-element.90), channel_id=1, source_target_pairs={{0,64},{64,128},{128,192},{192,256},{256,320},{320,384},{384,448},... | collective-permute-start | bytes 1544 | tf_op jit(solution)/shard_map/ppermute | solution.py:40
  209.7 14.0 %collective-permute-start.50 = (f32[4,1,64]{2,0,1:T(4,128)S(1)}, f32[4,1,64]{2,0,1:T(4,128)S(1)}, u32[]{:S(2)}, u32[]{:S(2)}) collective-permute-start(f32[4,1,64]{2,0,1:T(4,128)S(1)} %get-tuple-element.87), channel_id=1, source_target_pairs={{16,0},{32,16},{48,32},{17,1},{33,17},{49,33},{18,2},{34,18},{50,3... | collective-permute-start | bytes 3080 | tf_op jit(solution)/shard_map/ppermute | solution.py:41
  211.6 15.5 %collective-permute-start.51 = (f32[4,1,64]{2,0,1:T(4,128)S(1)}, f32[4,1,64]{2,0,1:T(4,128)S(1)}, u32[]{:S(2)}, u32[]{:S(2)}) collective-permute-start(f32[4,1,64]{2,0,1:T(4,128)S(1)} %get-tuple-element.86), channel_id=1, source_target_pairs={{0,16},{16,32},{32,48},{1,17},{17,33},{33,49},{2,18},{18,34},{34,5... | collective-permute-start | bytes 3080 | tf_op jit(solution)/shard_map/ppermute | solution.py:40
  215.0 14.3 %collective-permute-start.48 = (f32[1,2,64]{2,0,1:T(1,128)S(1)}, f32[1,2,64]{2,0,1:T(1,128)S(1)}, u32[]{:S(2)}, u32[]{:S(2)}) collective-permute-start(f32[1,2,64]{2,0,1:T(1,128)S(1)} %get-tuple-element.85), channel_id=1, source_target_pairs={{64,0},{128,64},{192,128},{256,192},{320,256},{384,320},{448,384},... | collective-permute-start | bytes 1544 | tf_op jit(solution)/shard_map/ppermute | solution.py:41
  216.9 12.4 %collective-permute-start.49 = (f32[1,2,64]{2,0,1:T(1,128)S(1)}, f32[1,2,64]{2,0,1:T(1,128)S(1)}, u32[]{:S(2)}, u32[]{:S(2)}) collective-permute-start(f32[1,2,64]{2,0,1:T(1,128)S(1)} %get-tuple-element.84), channel_id=1, source_target_pairs={{0,64},{64,128},{128,192},{192,256},{256,320},{320,384},{384,448},... | collective-permute-start | bytes 1544 | tf_op jit(solution)/shard_map/ppermute | solution.py:40
  229.5 14.0 %collective-permute-start.56 = (f32[4,1,64]{2,0,1:T(4,128)S(1)}, f32[4,1,64]{2,0,1:T(4,128)S(1)}, u32[]{:S(2)}, u32[]{:S(2)}) collective-permute-start(f32[4,1,64]{2,0,1:T(4,128)S(1)} %get-tuple-element.81), channel_id=1, source_target_pairs={{16,0},{32,16},{48,32},{17,1},{33,17},{49,33},{18,2},{34,18},{50,3... | collective-permute-start | bytes 3080 | tf_op jit(solution)/shard_map/ppermute | solution.py:41
  231.4 15.5 %collective-permute-start.57 = (f32[4,1,64]{2,0,1:T(4,128)S(1)}, f32[4,1,64]{2,0,1:T(4,128)S(1)}, u32[]{:S(2)}, u32[]{:S(2)}) collective-permute-start(f32[4,1,64]{2,0,1:T(4,128)S(1)} %get-tuple-element.80), channel_id=1, source_target_pairs={{0,16},{16,32},{32,48},{1,17},{17,33},{33,49},{2,18},{18,34},{34,5... | collective-permute-start | bytes 3080 | tf_op jit(solution)/shard_map/ppermute | solution.py:40
  234.8 14.3 %collective-permute-start.54 = (f32[1,2,64]{2,0,1:T(1,128)S(1)}, f32[1,2,64]{2,0,1:T(1,128)S(1)}, u32[]{:S(2)}, u32[]{:S(2)}) collective-permute-start(f32[1,2,64]{2,0,1:T(1,128)S(1)} %get-tuple-element.79), channel_id=1, source_target_pairs={{64,0},{128,64},{192,128},{256,192},{320,256},{384,320},{448,384},... | collective-permute-start | bytes 1544 | tf_op jit(solution)/shard_map/ppermute | solution.py:41
  236.7 12.4 %collective-permute-start.55 = (f32[1,2,64]{2,0,1:T(1,128)S(1)}, f32[1,2,64]{2,0,1:T(1,128)S(1)}, u32[]{:S(2)}, u32[]{:S(2)}) collective-permute-start(f32[1,2,64]{2,0,1:T(1,128)S(1)} %get-tuple-element.78), channel_id=1, source_target_pairs={{0,64},{64,128},{128,192},{192,256},{256,320},{320,384},{384,448},... | collective-permute-start | bytes 1544 | tf_op jit(solution)/shard_map/ppermute | solution.py:40
  249.2 14.0 %collective-permute-start.62 = (f32[4,1,64]{2,0,1:T(4,128)S(1)}, f32[4,1,64]{2,0,1:T(4,128)S(1)}, u32[]{:S(2)}, u32[]{:S(2)}) collective-permute-start(f32[4,1,64]{2,0,1:T(4,128)S(1)} %get-tuple-element.75), channel_id=1, source_target_pairs={{16,0},{32,16},{48,32},{17,1},{33,17},{49,33},{18,2},{34,18},{50,3... | collective-permute-start | bytes 3080 | tf_op jit(solution)/shard_map/ppermute | solution.py:41
  251.2 15.5 %collective-permute-start.63 = (f32[4,1,64]{2,0,1:T(4,128)S(1)}, f32[4,1,64]{2,0,1:T(4,128)S(1)}, u32[]{:S(2)}, u32[]{:S(2)}) collective-permute-start(f32[4,1,64]{2,0,1:T(4,128)S(1)} %get-tuple-element.74), channel_id=1, source_target_pairs={{0,16},{16,32},{32,48},{1,17},{17,33},{33,49},{2,18},{18,34},{34,5... | collective-permute-start | bytes 3080 | tf_op jit(solution)/shard_map/ppermute | solution.py:40
  254.6 14.3 %collective-permute-start.60 = (f32[1,2,64]{2,0,1:T(1,128)S(1)}, f32[1,2,64]{2,0,1:T(1,128)S(1)}, u32[]{:S(2)}, u32[]{:S(2)}) collective-permute-start(f32[1,2,64]{2,0,1:T(1,128)S(1)} %get-tuple-element.73), channel_id=1, source_target_pairs={{64,0},{128,64},{192,128},{256,192},{320,256},{384,320},{448,384},... | collective-permute-start | bytes 1544 | tf_op jit(solution)/shard_map/ppermute | solution.py:41
  256.5 12.4 %collective-permute-start.61 = (f32[1,2,64]{2,0,1:T(1,128)S(1)}, f32[1,2,64]{2,0,1:T(1,128)S(1)}, u32[]{:S(2)}, u32[]{:S(2)}) collective-permute-start(f32[1,2,64]{2,0,1:T(1,128)S(1)} %get-tuple-element.72), channel_id=1, source_target_pairs={{0,64},{64,128},{128,192},{192,256},{256,320},{320,384},{384,448},... | collective-permute-start | bytes 1544 | tf_op jit(solution)/shard_map/ppermute | solution.py:40
  269.0 14.0 %collective-permute-start.68 = (f32[4,1,64]{2,0,1:T(4,128)S(1)}, f32[4,1,64]{2,0,1:T(4,128)S(1)}, u32[]{:S(2)}, u32[]{:S(2)}) collective-permute-start(f32[4,1,64]{2,0,1:T(4,128)S(1)} %get-tuple-element.69), channel_id=1, source_target_pairs={{16,0},{32,16},{48,32},{17,1},{33,17},{49,33},{18,2},{34,18},{50,3... | collective-permute-start | bytes 3080 | tf_op jit(solution)/shard_map/ppermute | solution.py:41
  270.9 15.5 %collective-permute-start.69 = (f32[4,1,64]{2,0,1:T(4,128)S(1)}, f32[4,1,64]{2,0,1:T(4,128)S(1)}, u32[]{:S(2)}, u32[]{:S(2)}) collective-permute-start(f32[4,1,64]{2,0,1:T(4,128)S(1)} %get-tuple-element.68), channel_id=1, source_target_pairs={{0,16},{16,32},{32,48},{1,17},{17,33},{33,49},{2,18},{18,34},{34,5... | collective-permute-start | bytes 3080 | tf_op jit(solution)/shard_map/ppermute | solution.py:40
  274.3 14.3 %collective-permute-start.66 = (f32[1,2,64]{2,0,1:T(1,128)S(1)}, f32[1,2,64]{2,0,1:T(1,128)S(1)}, u32[]{:S(2)}, u32[]{:S(2)}) collective-permute-start(f32[1,2,64]{2,0,1:T(1,128)S(1)} %get-tuple-element.67), channel_id=1, source_target_pairs={{64,0},{128,64},{192,128},{256,192},{320,256},{384,320},{448,384},... | collective-permute-start | bytes 1544 | tf_op jit(solution)/shard_map/ppermute | solution.py:41
  276.3 12.4 %collective-permute-start.67 = (f32[1,2,64]{2,0,1:T(1,128)S(1)}, f32[1,2,64]{2,0,1:T(1,128)S(1)}, u32[]{:S(2)}, u32[]{:S(2)}) collective-permute-start(f32[1,2,64]{2,0,1:T(1,128)S(1)} %get-tuple-element.66), channel_id=1, source_target_pairs={{0,64},{64,128},{128,192},{192,256},{256,320},{320,384},{384,448},... | collective-permute-start | bytes 1544 | tf_op jit(solution)/shard_map/ppermute | solution.py:40
  283.1 5.6 %collective-permute-start.71 = (f32[4,2,1]{2,0,1:T(4,128)S(1)}, f32[4,2,1]{2,0,1:T(4,128)S(1)}, u32[]{:S(2)}, u32[]{:S(2)}) collective-permute-start(f32[4,2,1]{2,0,1:T(4,128)S(1)} %get-tuple-element.65), channel_id=1, source_target_pairs={{0,1},{1,2},{2,3},{3,4},{4,5},{5,6},{6,7},{7,8},{8,9},{9,10},{10,1... | collective-permute-start | bytes 104 | tf_op jit(solution)/shard_map/ppermute | solution.py:40
  290.8 14.1 %collective-permute-start.74 = (f32[8,1,128]{2,1,0:T(1,128)S(1)}, f32[8,1,128]{2,1,0:T(1,128)S(1)}, u32[]{:S(2)}, u32[]{:S(2)}) collective-permute-start(f32[8,1,128]{2,1,0:T(1,128)S(1)} %get-tuple-element.59), channel_id=1, source_target_pairs={{16,0},{32,16},{48,32},{17,1},{33,17},{49,33},{18,2},{34,18},{50,3... | collective-permute-start | bytes 12296 | tf_op jit(solution)/shard_map/ppermute | solution.py:41
  292.7 15.6 %collective-permute-start.75 = (f32[8,1,128]{2,1,0:T(1,128)S(1)}, f32[8,1,128]{2,1,0:T(1,128)S(1)}, u32[]{:S(2)}, u32[]{:S(2)}) collective-permute-start(f32[8,1,128]{2,1,0:T(1,128)S(1)} %get-tuple-element.58), channel_id=1, source_target_pairs={{0,16},{16,32},{32,48},{1,17},{17,33},{33,49},{2,18},{18,34},{34,5... | collective-permute-start | bytes 12296 | tf_op jit(solution)/shard_map/ppermute | solution.py:40
  296.1 14.5 %collective-permute-start.72 = (f32[1,4,128]{2,1,0:T(4,128)S(1)}, f32[1,4,128]{2,1,0:T(4,128)S(1)}, u32[]{:S(2)}, u32[]{:S(2)}) collective-permute-start(f32[1,4,128]{2,1,0:T(4,128)S(1)} %get-tuple-element.57), channel_id=1, source_target_pairs={{64,0},{128,64},{192,128},{256,192},{320,256},{384,320},{448,384},... | collective-permute-start | bytes 6152 | tf_op jit(solution)/shard_map/ppermute | solution.py:41
  298.0 12.6 %collective-permute-start.73 = (f32[1,4,128]{2,1,0:T(4,128)S(1)}, f32[1,4,128]{2,1,0:T(4,128)S(1)}, u32[]{:S(2)}, u32[]{:S(2)}) collective-permute-start(f32[1,4,128]{2,1,0:T(4,128)S(1)} %get-tuple-element.56), channel_id=1, source_target_pairs={{0,64},{64,128},{128,192},{192,256},{256,320},{320,384},{384,448},... | collective-permute-start | bytes 6152 | tf_op jit(solution)/shard_map/ppermute | solution.py:40
  304.9 5.7 %collective-permute-start.77 = (f32[8,4,1]{2,1,0:T(4,128)S(1)}, f32[8,4,1]{2,1,0:T(4,128)S(1)}, u32[]{:S(2)}, u32[]{:S(2)}) collective-permute-start(f32[8,4,1]{2,1,0:T(4,128)S(1)} %get-tuple-element.55), channel_id=1, source_target_pairs={{0,1},{1,2},{2,3},{3,4},{4,5},{5,6},{6,7},{7,8},{8,9},{9,10},{10,1... | collective-permute-start | bytes 392 | tf_op jit(solution)/shard_map/ppermute | solution.py:40
  322.9 14.1 %collective-permute-start.80 = (f32[16,1,256]{2,1,0:T(1,128)S(1)}, f32[16,1,256]{2,1,0:T(1,128)S(1)}, u32[]{:S(2)}, u32[]{:S(2)}) collective-permute-start(f32[16,1,256]{2,1,0:T(1,128)S(1)} %get-tuple-element.41), channel_id=1, source_target_pairs={{16,0},{32,16},{48,32},{17,1},{33,17},{49,33},{18,2},{34,18},{50,3... | collective-permute-start | bytes 49160 | tf_op jit(solution)/shard_map/ppermute | solution.py:41
  324.8 15.6 %collective-permute-start.81 = (f32[16,1,256]{2,1,0:T(1,128)S(1)}, f32[16,1,256]{2,1,0:T(1,128)S(1)}, u32[]{:S(2)}, u32[]{:S(2)}) collective-permute-start(f32[16,1,256]{2,1,0:T(1,128)S(1)} %get-tuple-element.40), channel_id=1, source_target_pairs={{0,16},{16,32},{32,48},{1,17},{17,33},{33,49},{2,18},{18,34},{34,5... | collective-permute-start | bytes 49160 | tf_op jit(solution)/shard_map/ppermute | solution.py:40
  328.2 15.0 %collective-permute-start.78 = (f32[1,8,256]{2,1,0:T(8,128)S(1)}, f32[1,8,256]{2,1,0:T(8,128)S(1)}, u32[]{:S(2)}, u32[]{:S(2)}) collective-permute-start(f32[1,8,256]{2,1,0:T(8,128)S(1)} %get-tuple-element.39), channel_id=1, source_target_pairs={{64,0},{128,64},{192,128},{256,192},{320,256},{384,320},{448,384},... | collective-permute-start | bytes 24584 | tf_op jit(solution)/shard_map/ppermute | solution.py:41
  330.1 13.1 %collective-permute-start.79 = (f32[1,8,256]{2,1,0:T(8,128)S(1)}, f32[1,8,256]{2,1,0:T(8,128)S(1)}, u32[]{:S(2)}, u32[]{:S(2)}) collective-permute-start(f32[1,8,256]{2,1,0:T(8,128)S(1)} %get-tuple-element.38), channel_id=1, source_target_pairs={{0,64},{64,128},{128,192},{192,256},{256,320},{320,384},{384,448},... | collective-permute-start | bytes 24584 | tf_op jit(solution)/shard_map/ppermute | solution.py:40
  337.0 6.2 %collective-permute-start.83 = (f32[16,8,1]{2,1,0:T(8,128)S(1)}, f32[16,8,1]{2,1,0:T(8,128)S(1)}, u32[]{:S(2)}, u32[]{:S(2)}) collective-permute-start(f32[16,8,1]{2,1,0:T(8,128)S(1)} %get-tuple-element.37), channel_id=1, source_target_pairs={{0,1},{1,2},{2,3},{3,4},{4,5},{5,6},{6,7},{7,8},{8,9},{9,10},{10,1... | collective-permute-start | bytes 1544 | tf_op jit(solution)/shard_map/ppermute | solution.py:40
  (41 other events, 406.5 us)
where the time goes:
time: 349 us; the launch traced here: 346 us
  starting transfers between devices  247 us (71%)
  local copies, waits for them, and re-layouts  39.6 us (11%)
  waiting for transfers between devices  32.7 us (9%)
  other arithmetic  24 us (7%)
    ppermute x30, starting transfers between devices, with_halo(): lax.ppermute(last, axis, up)  110 us
    ppermute x30, starting transfers between devices, with_halo(): lax.ppermute(initial, axis, [(b, a) for a, b in up])  64.6 us
    ppermute x12, starting transfers between devices, extended(): lax.ppermute(head, axis, [((i + 1) % count, i) for i in range(ends)])  38.6 us
    ppermute x12, starting transfers between devices, extended(): lax.ppermute(tail, axis, [(i, (i + 1) % count) for i in range(ends)])  34.1 us
    ppermute x30, waiting for transfers between devices, with_halo(): lax.ppermute(last, axis, up)  21.5 us
    reshape x3, local copies, waits for them, and re-layouts, coarsen(): cell_values.reshape(cell_values.shape[0] // 2, 2, cell_values.shape[1] //...  21.2 us
    reduce_sum x4, other arithmetic, coarsen(): return cell_values.reshape(cell_values.shape[0] // 2, 2, cell_values.shap...  8.39 us
    reshape x2, local copies, waits for them, and re-layouts, refine(): widened.reshape(2 * cell_values.shape[0], 2 * cell_values.shape[1], 2 * c...  8.01 us
  transfers between devices with their start and end apart: 84, of which 14 were waited for; matrix products, arithmetic and copies ran while one was open for 13% of the time, Pallas kernels for 0%

commit v1 on v0

v1 whole, which is shorter than its diff:
```python
import jax
import jax.numpy as jnp
from jax import lax
from jax.experimental import pallas as pl
from jax.experimental.pallas import tpu as pltpu
from jax.sharding import PartitionSpec as P

GAS_DENSITY = 0.001
RELAXATION = 0.8
KEEP = 1.0 - RELAXATION
COARSE_SWEEPS = 8
MESH = pl.DeviceIdType.MESH
CHUNK = 4
COPIES = 66


def iota(shape, axis):
    return lax.broadcasted_iota(jnp.int32, shape, axis)


def dot(a, b):
    return jnp.dot(a, b, precision=lax.Precision.HIGHEST, preferred_element_type=jnp.float32)


def kernel(src, mask, fac, out, V0, YS0, YH0, ZS0, ZH0, CX0, C0, INV0, DIAG0, R0,
           V1, YS1, YH1, ZS1, ZH1, G, SE, ZE, XB, XD, send_sem, recv_sem):
    nx, ny, nz = lax.axis_size("gx"), lax.axis_size("gy"), lax.axis_size("gz")
    sizes = {"gx": nx, "gy": ny, "gz": nz}
    at = {axis: lax.axis_index(axis) for axis in sizes}
    gy = at["gy"]
    f32 = jnp.float32

    def peer(axis, d):
        return {axis: lax.rem(at[axis] + (d + sizes[axis]), sizes[axis])}

    def exists(axis, d):
        place = at[axis] + d
        return (place >= 0) & (place < sizes[axis])

    copies = []

    def post(source, target, axis, d):
        k = len(copies)
        copy = pltpu.make_async_remote_copy(
            src_ref=source, dst_ref=target, send_sem=send_sem.at[k], recv_sem=recv_sem.at[k],
            device_id=peer(axis, d), device_id_type=MESH)
        copy.start()
        copies.append(copy)
        return copy

    sent = set()

    def arrived(group):
        for copy in group:
            copy.wait_recv()

    def left(group):
        for copy in group:
            copy.wait_send()
            sent.add(id(copy))

    def faces(V, YS, YH, ZS, ZH, k, planes):
        return [
            post(V.at[k, 1], V.at[k, planes + 1], "gx", -1),
            post(V.at[k, planes], V.at[k, 0], "gx", 1),
            post(YS.at[k, 0], YH.at[k, 1], "gy", -1),
            post(YS.at[k, 1], YH.at[k, 0], "gy", 1),
            post(ZS.at[k, 0], ZH.at[k, 1], "gz", -1),
            post(ZS.at[k, 1], ZH.at[k, 0], "gz", 1),
        ]

    def trim(V, YH, ZH, k, planes):
        V[k, 0] = jnp.where(exists("gx", -1), V[k, 0], 0.0)
        V[k, planes + 1] = jnp.where(exists("gx", 1), V[k, planes + 1], 0.0)
        for side, d in ((0, -1), (1, 1)):
            YH[k, side] = jnp.where(exists("gy", d), YH[k, side], 0.0)
            ZH[k, side] = jnp.where(exists("gz", d), ZH[k, side], 0.0)

    barrier = pltpu.get_barrier_semaphore()
    partners = [("gx", d) for d in (-1, 1, -2, 2, -3, 3)] + [("gy", d) for d in (1, 2, 3)] + [("gz", d) for d in (-1, 1)]
    for axis, d in partners:
        pl.semaphore_signal(barrier, inc=1, device_id=peer(axis, d), device_id_type=MESH)

    row8 = iota((8, 128), 0)
    lane8 = iota((8, 128), 1)

    row0 = iota((CHUNK, 8, 256), 1)
    lane0 = iota((CHUNK, 8, 256), 2)
    chunks = range(0, 16, CHUNK)

    def pack_y0(k, c, v):
        for i in range(CHUNK):
            YS0[k, 0, c + i:c + i + 1, :] = v[i, 0:1, :]
            YS0[k, 1, c + i:c + i + 1, :] = v[i, 7:8, :]

    def pack_z0(held, c, v):
        low, high = held
        for i in range(CHUNK):
            low = jnp.where(lane8 == c + i, jnp.broadcast_to(v[i, :, 0:1], (8, 128)), low)
            high = jnp.where(lane8 == c + i, jnp.broadcast_to(v[i, :, 255:256], (8, 128)), high)
        return low, high

    def spread_z0(packed, c):
        return jnp.stack([jnp.broadcast_to(packed[:, c + i:c + i + 1], (8, 256)) for i in range(CHUNK)])

    def rows_y0(ref, c):
        return jnp.stack([jnp.broadcast_to(ref[c + i:c + i + 1, :], (8, 256)) for i in range(CHUNK)])

    def shifts0(v, y_low, y_high, z_low, z_high):
        return (jnp.where(row0 == 7, y_high, pltpu.roll(v, 7, 1)),
                jnp.where(row0 == 0, y_low, pltpu.roll(v, 1, 1)),
                jnp.where(lane0 == 255, z_high, pltpu.roll(v, 255, 2)),
                jnp.where(lane0 == 0, z_low, pltpu.roll(v, 1, 2)))

    def halo0(k, c, zh):
        return (rows_y0(YH0.at[k, 0], c), rows_y0(YH0.at[k, 1], c), spread_z0(zh[0], c), spread_z0(zh[1], c))

    def around0(c, below, above, shifted):
        total = CX0[c:c + CHUNK] * below + CX0[c + 1:c + 1 + CHUNK] * above
        for n in range(4):
            total = total + C0[n, c:c + CHUNK] * shifted[n]
        return total

    zeros8 = jnp.zeros((8, 128), f32)
    held = (zeros8, zeros8)
    for c in chunks:
        rho = jnp.where(mask[c:c + CHUNK] == 1, GAS_DENSITY, 1.0) * fac[c:c + CHUNK]
        V0[0, 1 + c:1 + c + CHUNK] = rho
        pack_y0(0, c, rho)
        held = pack_z0(held, c, rho)
    ZS0[0, 0], ZS0[0, 1] = held
    pl.semaphore_wait(barrier, len(partners))
    rho0_faces = faces(V0, YS0, YH0, ZS0, ZH0, 0, 16)

    row1 = iota((8, 8, 128), 1)
    lane1 = iota((8, 8, 128), 2)
    own1 = (row1 >= 2) & (row1 < 6)
    pairs0 = (lax.shift_right_logical(iota((256, 128), 0), 1) == iota((256, 128), 1)).astype(f32)
    pairs1 = (lax.shift_right_logical(iota((128, 128), 0), 1) == iota((128, 128), 1)).astype(f32)

    def down0(field):
        t = field.reshape(8, 2, 8, 256)
        t = t[:, 0] + t[:, 1]
        t = dot(t.reshape(64, 256), pairs0).reshape(8, 8, 128)
        t = t + pltpu.roll(t, 7, 1)
        t = jnp.where(row1 == 2, pltpu.roll(t, 2, 1),
                      jnp.where(row1 == 3, pltpu.roll(t, 1, 1), jnp.where(row1 == 4, t, pltpu.roll(t, 7, 1))))
        return jnp.where(own1, t, 0.0)

    def down1(field):
        t = field.reshape(4, 2, 8, 128)
        t = t[:, 0] + t[:, 1]
        t = t + pltpu.roll(t, 7, 1)
        packed = zeros8
        for x in range(4):
            for half in range(2):
                shift = (2 * x + half - 2 - 2 * half) % 8
                moved = pltpu.roll(t[x], shift, 0) if shift else t[x]
                packed = jnp.where(row8 == 2 * x + half, moved, packed)
        return dot(packed, pairs1)

    def stage1(k, v):
        V1[k, 1:9] = v
        low, high = zeros8, zeros8
        for p in range(8):
            YS1[k, 0, p:p + 1, :] = v[p, 2:3, :]
            YS1[k, 1, p:p + 1, :] = v[p, 5:6, :]
            low = jnp.where(lane8 == p, jnp.broadcast_to(v[p, :, 0:1], (8, 128)), low)
            high = jnp.where(lane8 == p, jnp.broadcast_to(v[p, :, 127:128], (8, 128)), high)
        ZS1[k, 0], ZS1[k, 1] = low, high
        return faces(V1, YS1, YH1, ZS1, ZH1, k, 8)

    def settle1(k, group):
        arrived(group)
        left(group)
        trim(V1, YH1, ZH1, k, 8)
        for p in range(8):
            V1[k, 1 + p] = jnp.where(row8 == 1, YH1[k, 0, p:p + 1, :], jnp.where(row8 == 6, YH1[k, 1, p:p + 1, :], V1[k, 1 + p]))

    def spread_z1(k):
        low, high = ZH1[k, 0], ZH1[k, 1]
        return (jnp.stack([jnp.broadcast_to(low[:, p:p + 1], (8, 128)) for p in range(8)]),
                jnp.stack([jnp.broadcast_to(high[:, p:p + 1], (8, 128)) for p in range(8)]))

    def shifts1(v, z_low, z_high):
        return (pltpu.roll(v, 7, 1), pltpu.roll(v, 1, 1),
                jnp.where(lane1 == 127, z_high, pltpu.roll(v, 127, 2)),
                jnp.where(lane1 == 0, z_low, pltpu.roll(v, 1, 2)))

    def gather_y2(k, packed):
        G[k, gy] = packed
        return [post(G.at[k, gy], G.at[k, gy], "gy", d) for d in (1, 2, 3)]

    def gather_z2(k):
        for x in range(4):
            t = zeros8
            for q in range(4):
                shift = (2 * (q - x)) % 8
                moved = pltpu.roll(G[k, q], shift, 0) if shift else G[k, q]
                t = jnp.where(lax.shift_right_logical(row8, 1) == q, moved, t)
            SE[k, x] = t
        return [post(SE.at[k], ZE.at[k, 1], "gz", -1), post(SE.at[k], ZE.at[k, 0], "gz", 1)]

    def widen_z2(k):
        lane = iota((4, 8, 128), 2)
        low = jnp.where(exists("gz", -1), ZE[k, 0], 0.0)
        high = jnp.where(exists("gz", 1), ZE[k, 1], 0.0)
        return jnp.where(lane < 64, SE[k], pltpu.roll(jnp.where(lane < 32, high, low), 64, 2))

    rho1 = 0.125 * down0(V0[0, 1:17])
    rho1_faces = stage1(0, rho1)
    rho2_y = gather_y2(0, 0.125 * down1(rho1))

    arrived(rho0_faces)
    trim(V0, YH0, ZH0, 0, 16)
    for c in range(17):
        CX0[c] = 2.0 / (V0[0, c] + V0[0, c + 1])
    zh = (ZH0[0, 0], ZH0[0, 1])
    held = (zeros8, zeros8)
    for c in chunks:
        rho = V0[0, 1 + c:1 + c + CHUNK]
        shifted = shifts0(rho, *halo0(0, c, zh))
        diag = CX0[c:c + CHUNK] + CX0[c + 1:c + 1 + CHUNK]
        for n in range(4):
            coupling = 2.0 / (rho + shifted[n])
            C0[n, c:c + CHUNK] = coupling
            diag = diag + coupling
        inv = RELAXATION / diag
        DIAG0[c:c + CHUNK] = diag
        INV0[c:c + CHUNK] = inv
        v = inv * src[c:c + CHUNK]
        V0[1, 1 + c:1 + c + CHUNK] = v
        pack_y0(1, c, v)
        held = pack_z0(held, c, v)
    ZS0[1, 0], ZS0[1, 1] = held
    v1_faces = faces(V0, YS0, YH0, ZS0, ZH0, 1, 16)

    arrived(rho2_y)
    rho2_z = gather_z2(0)

    settle1(0, rho1_faces)
    rho = V1[0, 1:9]
    x_low1 = 2.0 / (rho + V1[0, 0:8])
    x_high1 = 2.0 / (rho + V1[0, 2:10])
    around1_c = [2.0 / (rho + other) for other in shifts1(rho, *spread_z1(0))]
    diag1 = x_low1 + x_high1 + ((around1_c[0] + around1_c[1]) + (around1_c[2] + around1_c[3]))
    inv1 = RELAXATION / diag1

    def around1(k_or_v, z_low, z_high):
        v = k_or_v
        total = x_low1 * v[0:8] + x_high1 * v[2:10]
        for coupling, other in zip(around1_c, shifts1(v[1:9], z_low, z_high)):
            total = total + coupling * other
        return total

    arrived(v1_faces)
    trim(V0, YH0, ZH0, 1, 16)
    zh = (ZH0[1, 0], ZH0[1, 1])
    held = (zeros8, zeros8)
    for c in chunks:
        v = V0[1, 1 + c:1 + c + CHUNK]
        total = around0(c, V0[1, c:c + CHUNK], V0[1, c + 2:c + 2 + CHUNK], shifts0(v, *halo0(1, c, zh)))
        v = KEEP * v + INV0[c:c + CHUNK] * (src[c:c + CHUNK] + total)
        V0[2, 1 + c:1 + c + CHUNK] = v
        pack_y0(2, c, v)
        held = pack_z0(held, c, v)
    ZS0[2, 0], ZS0[2, 1] = held
    v2_faces = faces(V0, YS0, YH0, ZS0, ZH0, 2, 16)

    arrived(rho2_z)
    XD[9:13] = widen_z2(0)
    rho2_x = [post(XD.at[9:13], XD.at[9 - 4 * d:13 - 4 * d], "gx", d) for d in (-2, -1, 1, 2)]
    rho2_x += [post(XD.at[12], XD.at[0], "gx", 3), post(XD.at[9], XD.at[21], "gx", -3)]

    arrived(v2_faces)
    trim(V0, YH0, ZH0, 2, 16)
    zh = (ZH0[2, 0], ZH0[2, 1])
    for c in chunks:
        v = V0[2, 1 + c:1 + c + CHUNK]
        total = around0(c, V0[2, c:c + CHUNK], V0[2, c + 2:c + 2 + CHUNK], shifts0(v, *halo0(2, c, zh)))
        R0[c:c + CHUNK] = src[c:c + CHUNK] + total - DIAG0[c:c + CHUNK] * v
    b1 = 0.5 * down0(R0[...])
    w1_faces = stage1(1, jnp.where(own1, inv1 * b1, 0.0))

    arrived(rho2_x)
    for d in (-2, -1, 1, 2):
        XD[9 - 4 * d:13 - 4 * d] = jnp.where(exists("gx", -d), XD[9 - 4 * d:13 - 4 * d], 0.0)
    XD[0] = jnp.where(exists("gx", -3), XD[0], 0.0)
    XD[21] = jnp.where(exists("gx", 3), XD[21], 0.0)

    def coupling2(a, b):
        total = a + b
        return jnp.where(total > 0.0, 2.0 / total, 0.0)

    row2 = iota((20, 8, 128), 1)
    rho = XD[1:21]
    cx2 = coupling2(XD[0:21], XD[1:22])
    y_up = coupling2(rho, jnp.where(row2 == 7, 0.0, pltpu.roll(rho, 7, 1)))
    y_down = coupling2(rho, jnp.where(row2 == 0, 0.0, pltpu.roll(rho, 1, 1)))
    z_up = coupling2(rho, pltpu.roll(rho, 127, 2))
    z_down = coupling2(rho, pltpu.roll(rho, 1, 2))
    diag2 = cx2[0:20] + cx2[1:21] + ((y_up + y_down) + (z_up + z_down))
    inv2 = jnp.where(rho > 0.0, RELAXATION / diag2, 0.0)
    y_up = jnp.where(row2 == 7, 0.0, y_up)
    y_down = jnp.where(row2 == 0, 0.0, y_down)

    settle1(1, w1_faces)
    w = V1[1]
    w2 = KEEP * w[1:9] + inv1 * (b1 + around1(w, *spread_z1(1)))
    w2_faces = stage1(2, jnp.where(own1, w2, 0.0))
    settle1(2, w2_faces)
    w = V1[2]
    w_low, w_high = spread_z1(2)
    r1 = jnp.where(own1, b1 + around1(w, w_low, w_high) - diag1 * w[1:9], 0.0)

    arrived(gather_y2(1, 0.5 * down1(r1)))
    arrived(gather_z2(1))
    XB[8:12] = widen_z2(1)
    arrived([post(XB.at[8:12], XB.at[8 - 4 * d:12 - 4 * d], "gx", d) for d in (-2, -1, 1, 2)])
    for d in (-2, -1, 1, 2):
        XB[8 - 4 * d:12 - 4 * d] = jnp.where(exists("gx", -d), XB[8 - 4 * d:12 - 4 * d], 0.0)
    b2 = XB[...]
    v = inv2 * b2
    for k in range(1, COARSE_SWEEPS):
        a, z = k, 20 - k
        here = v[1:-1]
        total = cx2[a:z] * v[:-2] + cx2[a + 1:z + 1] * v[2:]
        total = total + y_up[a:z] * pltpu.roll(here, 7, 1) + y_down[a:z] * pltpu.roll(here, 1, 1)
        total = total + z_up[a:z] * pltpu.roll(here, 127, 2) + z_down[a:z] * pltpu.roll(here, 1, 2)
        v = KEEP * here + inv2[a:z] * (b2[a:z] + total)

    row6 = iota((6, 8, 128), 1)
    s = pltpu.roll(v, lax.rem(2 - 2 * gy + 8, 8), 1)
    t = jnp.where(row6 <= 2, s, jnp.where(row6 <= 4, pltpu.roll(s, 1, 1), pltpu.roll(s, 2, 1)))
    first = jnp.where(exists("gy", -1), 1, 2)
    last = jnp.where(exists("gy", 1), 6, 5)
    t = jnp.where((row6 >= first) & (row6 <= last), t, 0.0)
    from_lane = iota((128, 384), 0)
    to_lane = iota((128, 384), 1)
    wanted = jnp.where(to_lane < 128, lax.shift_right_logical(to_lane, 1), jnp.where(to_lane < 256, 64, 127))
    t = dot(t.reshape(48, 128), (from_lane == wanted).astype(f32)).reshape(6, 8, 384)
    w3 = V1[2] + jnp.stack([t[j, :, 0:128] for j in (0, 1, 1, 2, 2, 3, 3, 4, 4, 5)])
    w_high = w_high + jnp.stack([t[j, :, 128:256] for j in (1, 1, 2, 2, 3, 3, 4, 4)])
    w_low = w_low + jnp.stack([t[j, :, 256:384] for j in (1, 1, 2, 2, 3, 3, 4, 4)])
    e1 = KEEP * w3[1:9] + inv1 * (b1 + around1(w3, w_low, w_high))
    e1_faces = stage1(3, jnp.where(own1, e1, 0.0))
    settle1(3, e1_faces)

    def grow_y(t, axis):
        row = iota(t.shape, axis)
        up, down = pltpu.roll(t, 7, axis), pltpu.roll(t, 1, axis)
        t = jnp.where((row == 3) | (row == 4), t, jnp.where(row < 3, up, down))
        return jnp.where(row == 0, pltpu.roll(up, 7, axis), jnp.where(row == 7, pltpu.roll(down, 1, axis), t))

    pairs = (iota((128, 256), 0) == lax.shift_right_logical(iota((128, 256), 1), 1)).astype(f32)
    e = dot(V1[3].reshape(80, 128), pairs).reshape(10, 8, 256)
    grown = grow_y(e, 1)
    ez = (grow_y(ZH1[3, 0], 0), grow_y(ZH1[3, 1], 0))
    left(v2_faces)
    V0[2, 0] = V0[2, 0] + grown[0]
    V0[2, 17] = V0[2, 17] + grown[9]
    for i in range(16):
        V0[2, 1 + i] = V0[2, 1 + i] + grown[1 + i // 2]
        YH0[2, 0, i:i + 1, :] = YH0[2, 0, i:i + 1, :] + e[1 + i // 2, 1:2, :]
        YH0[2, 1, i:i + 1, :] = YH0[2, 1, i:i + 1, :] + e[1 + i // 2, 6:7, :]
    for c in chunks:
        v = V0[2, 1 + c:1 + c + CHUNK]
        y_low, y_high, z_low, z_high = halo0(2, c, zh)
        coarse = [jnp.stack([jnp.broadcast_to(side[:, (c + i) // 2:(c + i) // 2 + 1], (8, 256)) for i in range(CHUNK)])
                  for side in ez]
        total = around0(c, V0[2, c:c + CHUNK], V0[2, c + 2:c + 2 + CHUNK],
                        shifts0(v, y_low, y_high, z_low + coarse[0], z_high + coarse[1]))
        out[c:c + CHUNK] = KEEP * v + INV0[c:c + CHUNK] * (src[c:c + CHUNK] + total)

    left([copy for copy in copies if id(copy) not in sent])


def shards(source, phase_mask, density_factor):
    f32 = jnp.float32
    vmem = pl.BlockSpec(memory_space=pltpu.VMEM)
    return pl.pallas_call(
        kernel,
        out_shape=jax.ShapeDtypeStruct((16, 8, 256), f32),
        in_specs=[vmem] * 3,
        out_specs=vmem,
        scratch_shapes=[
            pltpu.VMEM((3, 18, 8, 256), f32),
            pltpu.VMEM((3, 2, 16, 256), f32),
            pltpu.VMEM((3, 2, 16, 256), f32),
            pltpu.VMEM((3, 2, 8, 128), f32),
            pltpu.VMEM((3, 2, 8, 128), f32),
            pltpu.VMEM((17, 8, 256), f32),
            pltpu.VMEM((4, 16, 8, 256), f32),
            pltpu.VMEM((16, 8, 256), f32),
            pltpu.VMEM((16, 8, 256), f32),
            pltpu.VMEM((16, 8, 256), f32),
            pltpu.VMEM((4, 10, 8, 128), f32),
            pltpu.VMEM((4, 2, 8, 128), f32),
            pltpu.VMEM((4, 2, 8, 128), f32),
            pltpu.VMEM((4, 2, 8, 128), f32),
            pltpu.VMEM((4, 2, 8, 128), f32),
            pltpu.VMEM((2, 4, 8, 128), f32),
            pltpu.VMEM((2, 4, 8, 128), f32),
            pltpu.VMEM((2, 2, 4, 8, 128), f32),
            pltpu.VMEM((20, 8, 128), f32),
            pltpu.VMEM((22, 8, 128), f32),
            pltpu.SemaphoreType.DMA((COPIES,)),
            pltpu.SemaphoreType.DMA((COPIES,)),
        ],
        compiler_params=pltpu.CompilerParams(collective_id=0, has_side_effects=True),
        name="vcycle",
    )(source, phase_mask, density_factor)


def solution(mesh):
    spec = P("gx", "gy", "gz")
    return jax.shard_map(shards, mesh=mesh, in_specs=(spec,) * 3, out_specs=spec, check_vma=False)
```

time: 349 us -> 57.2 us (0.16)
  the two profiles are of different devices: /device:TPU:795 before, /device:TPU:1 now
where the time goes in v1:
time: 57.2 us; the launch traced here: 57 us
  Pallas kernels  55.4 us (97%)
  local copies, waits for them, and re-layouts  1.57 us (3%)
    pallas_call x1, Pallas kernels, shards(): pl.pallas_call(kernel, out_shape=jax.ShapeDtypeStruct((16, 8, 256), f32),...  55.4 us
    unnamed x1, local copies, waits for them, and re-layouts  1.57 us

profile of v1, /device:TPU:1, one launch (start us, length us, event | category | flops | bytes accessed | tf_op | source)
XLA Modules:
  0.0 57.0 jit_solution(6164768710150698951)
XLA Ops:
  0.0 55.4 %vcycle.1 = f32[16,8,256]{2,1,0:T(8,128)} custom-call(f32[16,8,256]{2,1,0:T(8,128)} %src.1, s32[16,8,256]{2,1,0:T(8,128)} %mask.1, f32[16,8,256]{2,1,0:T(8,128)} %fac.1), custom_call_target="tpu_custom_call" | custom-call | tf_op jit(solution)/shard_map/vcycle/pallas_call | solution.py:381
  55.4 1.6 %copy.5 = f32[16,8,256]{2,1,0:T(8,128)} copy(f32[16,8,256]{2,1,0:T(8,128)} %vcycle.1) | data formatting | bytes 262144

commit v2 on v0

v2 whole, which is shorter than its diff:
```python
import jax
import jax.numpy as jnp
from jax import lax
from jax.experimental import pallas as pl
from jax.experimental.pallas import tpu as pltpu
from jax.sharding import PartitionSpec as P

GAS_DENSITY = 0.001
RELAXATION = 0.8
KEEP = 1.0 - RELAXATION
COARSE_SWEEPS = 8
MESH = pl.DeviceIdType.MESH
CHUNK = 2
COPIES = 66
TINY = 1e-30
AXES = ("gx", "gy", "gz")
SIDES = [(a, b) for a in (-1, 0, 1) for b in (-1, 0, 1) if a or b]


def iota(shape, axis):
    return lax.broadcasted_iota(jnp.int32, shape, axis)


def dot(a, b):
    high = a.astype(jnp.bfloat16)
    rest = a - high.astype(jnp.float32)
    middle = rest.astype(jnp.bfloat16)
    low = (rest - middle.astype(jnp.float32)).astype(jnp.bfloat16)
    return sum(jnp.dot(part, b, preferred_element_type=jnp.float32) for part in (low, middle, high))


def ones_where(condition):
    return jnp.where(condition, 1.0, 0.0).astype(jnp.bfloat16)


def turn(x, shift, axis):
    shift %= x.shape[axis]
    return pltpu.roll(x, shift, axis) if shift else x


def coupling(a, b):
    return 2.0 / jnp.maximum(a + b, TINY)


def grow(t, axis):
    row = iota(t.shape, axis)
    moved = [t] + [pltpu.roll(t, n, axis) for n in (1, 2, 3, 4)]
    low = jnp.where(row < 1, moved[0], jnp.where(row < 3, moved[1], moved[2]))
    high = jnp.where(row < 5, moved[2], jnp.where(row < 7, moved[3], moved[4]))
    return jnp.where(row < 4, low, high)


def kernel(src, mask, fac, out, V0, SRC, YS0, YH0, ZS, ZH, HX, HY, CX0, C0, INV0, DIAG0,
           S1, H1, RHO1, CX1, C1, INV1, DIAG1, B1, W1, W2, E1, G, GB, XD, send_sem, recv_sem):
    f32 = jnp.float32
    sizes = {axis: lax.axis_size(axis) for axis in AXES}
    at = {axis: lax.axis_index(axis) for axis in AXES}
    gx, gy = at["gx"], at["gy"]

    def peer(way):
        return {axis: lax.rem(at[axis] + (d + sizes[axis]), sizes[axis]) for axis, d in way.items() if d}

    def exists(axis, d):
        place = at[axis] + d
        return (place >= 0) & (place < sizes[axis])

    above, below = exists("gz", 1), exists("gz", -1)
    copies = []

    def ready(source, target, way):
        k = len(copies)
        copy = pltpu.make_async_remote_copy(
            src_ref=source, dst_ref=target, send_sem=send_sem.at[k], recv_sem=recv_sem.at[k],
            device_id=peer(way), device_id_type=MESH)
        copies.append(copy)
        return copy

    def post(source, target, way):
        copy = ready(source, target, way)
        copy.start()
        return copy

    def arrived(group):
        for copy in group:
            copy.wait_recv()

    sent = set()

    def left(group):
        for copy in group:
            copy.wait_send()
            sent.add(id(copy))

    barrier = pltpu.get_barrier_semaphore()
    steady = [{"gx": a, "gy": b} for a in (-2, -1, 0, 1, 2) for b in (0, 1, 2, 3) if a or b] + [{"gx": -3}, {"gx": 3}]
    across = [{}, {"gx": -1}, {"gx": 1}, {"gy": -1}, {"gy": 1}]
    for way in steady:
        pl.semaphore_signal(barrier, inc=1, device_id=peer(way), device_id_type=MESH)
    for d, there in ((-1, below), (1, above)):
        ids = [peer({**way, "gz": d}) for way in across]

        @pl.when(there)
        def _():
            for other in ids:
                pl.semaphore_signal(barrier, inc=1, device_id=other, device_id_type=MESH)

    lane16 = iota((16, 8, 128), 2)
    row0 = iota((CHUNK, 8, 384), 1)
    chunks = range(0, 16, CHUNK)

    def pack_y0(k, c, v):
        n = v.shape[-1]
        for i in range(v.shape[0]):
            YS0[k, 0, c + i:c + i + 1, 0:n] = v[i, 0:1, :]
            YS0[k, 1, c + i:c + i + 1, 0:n] = v[i, 7:8, :]

    def halo0(k, c):
        return [jnp.stack([jnp.broadcast_to(YH0[k, side, c + i:c + i + 1, :], (8, 384)) for i in range(CHUNK)])
                for side in (0, 1)]

    def shifts0(v, y_low, y_high):
        return (jnp.where(row0 == 7, y_high, pltpu.roll(v, 7, 1)), jnp.where(row0 == 0, y_low, pltpu.roll(v, 1, 1)),
                pltpu.roll(v, 383, 2), pltpu.roll(v, 1, 2))

    def around0(k, c):
        v = V0[k, 1 + c:1 + c + CHUNK]
        total = CX0[c:c + CHUNK] * V0[k, c:c + CHUNK] + CX0[c + 1:c + 1 + CHUNK] * V0[k, c + 2:c + 2 + CHUNK]
        for n, other in enumerate(shifts0(v, *halo0(k, c))):
            total = total + C0[n, c:c + CHUNK] * other
        return v, total

    def faces0(k):
        return [post(V0.at[k, 1], V0.at[k, 17], {"gx": -1}), post(V0.at[k, 16], V0.at[k, 0], {"gx": 1}),
                post(YS0.at[k, 0], YH0.at[k, 1], {"gy": -1}), post(YS0.at[k, 1], YH0.at[k, 0], {"gy": 1})]

    def trim0(k):
        V0[k, 0] = jnp.where(exists("gx", -1), V0[k, 0], 0.0)
        V0[k, 17] = jnp.where(exists("gx", 1), V0[k, 17], 0.0)
        YH0[k, 0] = jnp.where(exists("gy", -1), YH0[k, 0], 0.0)
        YH0[k, 1] = jnp.where(exists("gy", 1), YH0[k, 1], 0.0)

    rho = jnp.where(mask[...] == 1, GAS_DENSITY, 1.0) * fac[...]
    V0[0, 1:17, :, 0:256] = rho
    source = src[...]
    ZS[0] = jnp.where(lane16 < 64, rho[:, :, 0:128], pltpu.roll(source[:, :, 0:128], 64, 2))
    ZS[1] = jnp.where(lane16 < 64, pltpu.roll(rho[:, :, 128:256], 64, 2), source[:, :, 128:256])
    pack_y0(0, 0, rho)
    SRC[:, :, 0:256] = source
    two = jnp.where(above, 1, 0) + jnp.where(below, 1, 0)
    pl.semaphore_wait(barrier, len(steady) + len(across) * two)

    low, high = pl.ds(0, 128), pl.ds(128, 128)
    to_below = [ready(ZS.at[0], ZH.at[1], {"gz": -1}),
                ready(V0.at[0, 1, :, low], HX.at[1, 1], {"gx": -1, "gz": -1}),
                ready(V0.at[0, 16, :, low], HX.at[0, 1], {"gx": 1, "gz": -1}),
                ready(YS0.at[0, 0, :, low], HY.at[1, 1], {"gy": -1, "gz": -1}),
                ready(YS0.at[0, 1, :, low], HY.at[0, 1], {"gy": 1, "gz": -1})]
    to_above = [ready(ZS.at[1], ZH.at[0], {"gz": 1}),
                ready(V0.at[0, 1, :, high], HX.at[1, 0], {"gx": -1, "gz": 1}),
                ready(V0.at[0, 16, :, high], HX.at[0, 0], {"gx": 1, "gz": 1}),
                ready(YS0.at[0, 0, :, high], HY.at[1, 0], {"gy": -1, "gz": 1}),
                ready(YS0.at[0, 1, :, high], HY.at[0, 0], {"gy": 1, "gz": 1})]
    for group, there in ((to_below, below), (to_above, above)):
        @pl.when(there)
        def _():
            for copy in group:
                copy.start()
    both = pl.ds(0, 256)
    rho0_faces = [post(V0.at[0, 1, :, both], V0.at[0, 17, :, both], {"gx": -1}),
                  post(V0.at[0, 16, :, both], V0.at[0, 0, :, both], {"gx": 1}),
                  post(YS0.at[0, 0, :, both], YH0.at[0, 1, :, both], {"gy": -1}),
                  post(YS0.at[0, 1, :, both], YH0.at[0, 0, :, both], {"gy": 1})]

    a, b = lax.shift_right_logical(iota((384, 256), 0), 1), iota((384, 256), 1)
    pairs0 = ones_where(b == jnp.where(a < 160, a, a + 64))
    pairs1 = ones_where(lax.shift_right_logical(iota((256, 128), 0), 1) == iota((256, 128), 1))
    a, b = iota((256, 384), 0), lax.shift_right_logical(iota((256, 384), 1), 1)
    spread0 = ones_where(a == jnp.where(b < 160, b, b + 64))
    spread1 = ones_where(iota((128, 256), 0) == lax.shift_right_logical(iota((128, 256), 1), 1))

    arrived(rho0_faces)
    for group, there in ((to_below, above), (to_above, below)):
        @pl.when(there)
        def _():
            arrived(group)
    for group, there in ((to_below, below), (to_above, above)):
        @pl.when(there)
        def _():
            left(group)

    ring = slice(256, 384)
    up, down = jnp.where(above, ZH[1], 0.0), jnp.where(below, ZH[0], 0.0)
    V0[0, 1:17, :, ring] = jnp.where(lane16 < 64, up, pltpu.roll(down, 64, 2))
    SRC[:, :, ring] = jnp.where(lane16 < 64, pltpu.roll(up, 64, 2), down)
    lane8, lane2 = iota((8, 128), 1), iota((16, 128), 1)
    for side in (0, 1):
        V0[0, 17 * side, :, ring] = jnp.where(
            lane8 < 64, jnp.where(above, HX[side, 1], 0.0), jnp.where(below, HX[side, 0], 0.0))
        YH0[0, side, :, ring] = jnp.where(
            lane2 < 64, jnp.where(above, HY[side, 1], 0.0), jnp.where(below, HY[side, 0], 0.0))
    trim0(0)

    for c in range(17):
        CX0[c] = coupling(V0[0, c], V0[0, c + 1])
    for c in chunks:
        rho = V0[0, 1 + c:1 + c + CHUNK]
        diag = CX0[c:c + CHUNK] + CX0[c + 1:c + 1 + CHUNK]
        for n, other in enumerate(shifts0(rho, *halo0(0, c))):
            between = coupling(rho, other)
            C0[n, c:c + CHUNK] = between
            diag = diag + between
        inv = jnp.where(rho > 0.0, RELAXATION / diag, 0.0)
        DIAG0[c:c + CHUNK] = diag
        INV0[c:c + CHUNK] = inv
        v = inv * SRC[c:c + CHUNK]
        V0[1, 1 + c:1 + c + CHUNK] = v
        pack_y0(1, c, v)
    v1_faces = faces0(1)

    row8 = iota((8, 256), 0)
    row8s = iota((8, 128), 0)

    def down0(plane):
        t = jnp.concatenate([plane(2 * p) + plane(2 * p + 1) for p in range(8)], axis=0)
        t = dot(t, pairs0).reshape(8, 8, 256)
        t = t + pltpu.roll(t, 7, 1)
        row = iota((8, 8, 256), 1)
        t = jnp.where(row < 1, t, jnp.where(row < 2, pltpu.roll(t, 7, 1), jnp.where(row < 3, pltpu.roll(t, 6, 1), pltpu.roll(t, 5, 1))))
        return [jnp.where(row8 < 4, t[2 * j], pltpu.roll(t[2 * j + 1], 4, 0)) for j in range(4)]

    def slot(a, b):
        return SIDES.index((a, b))

    def exchange1(k, packed):
        for j in range(4):
            S1[k, j] = packed[j]
        group = []
        for a, b in ((1, 0), (-1, 0), (0, 1), (0, -1), (1, 1), (1, -1), (-1, 1), (-1, -1)):
            some = {1: pl.ds(2, 2), -1: pl.ds(0, 2), 0: pl.ds(0, 4)}[a]
            group.append(post(S1.at[k, some], H1.at[k, slot(-a, -b), some], {"gx": a, "gy": b}))
        return group

    def unpack1(k, target, first, last, offset):
        for p in range(first, last):
            a = p // 8
            j, half = (p % 8) // 2, p % 2

            def block(b):
                if not a and not b:
                    return S1[k, j]
                return jnp.where(exists("gx", a) & exists("gy", b), H1[k, slot(a, b), j], 0.0)

            target[p - offset, 0:8] = jnp.where(row8 < 4, turn(block(0), -4 * half, 0), turn(block(1), 4 - 4 * half, 0))
            target[p - offset, 8:16] = jnp.where(row8 < 4, 0.0, turn(block(-1), 4 - 4 * half, 0))

    def shifts1(v):
        return pltpu.roll(v, 15, 0), pltpu.roll(v, 1, 0), pltpu.roll(v, 255, 1), pltpu.roll(v, 1, 1)

    def around1(V, p, base):
        v = V[p - base]
        total = CX1[p + 3] * V[p - 1 - base] + CX1[p + 4] * V[p + 1 - base]
        for n, other in enumerate(shifts1(v)):
            total = total + C1[n, p + 3] * other
        return v, total

    def down1(plane):
        packed = jnp.zeros((8, 256), f32)
        for x in range(4):
            t = plane(2 * x) + plane(2 * x + 1)
            t = t + pltpu.roll(t, 7, 0)
            for half in range(2):
                packed = jnp.where(row8 == 2 * x + half, turn(t, 2 * x - half, 0), packed)
        return dot(packed, pairs1)

    packed1 = [0.125 * t for t in down0(lambda p: V0[0, 1 + p])]
    rho1_copies = exchange1(0, packed1)
    G[gy] = 0.125 * down1(lambda p: packed1[p // 2] if p % 2 == 0 else pltpu.roll(packed1[p // 2], 4, 0))
    rho2_y = [post(G.at[gy], G.at[gy], {"gy": d}) for d in (1, 2, 3)]

    arrived(v1_faces)
    trim0(1)
    for c in chunks:
        v, total = around0(1, c)
        v = KEEP * v + INV0[c:c + CHUNK] * (SRC[c:c + CHUNK] + total)
        V0[2, 1 + c:1 + c + CHUNK] = v
        pack_y0(2, c, v)
    v2_faces = faces0(2)

    def rows_of(blocks):
        planes = []
        for x in range(4):
            t = turn(blocks[0], -2 * x, 0)
            for q in (1, 2, 3):
                t = jnp.where(row8s < 2 * q, t, turn(blocks[q], 2 * (q - x), 0))
            planes.append(t)
        return planes

    arrived(rho2_y)
    for x, t in enumerate(rows_of([G[q] for q in range(4)])):
        XD[9 + x] = t
    rho2_x = [post(XD.at[9:13], XD.at[9 - 4 * d:13 - 4 * d], {"gx": d}) for d in (-2, -1, 1, 2)]
    rho2_x += [post(XD.at[12], XD.at[0], {"gx": 3}), post(XD.at[9], XD.at[21], {"gx": -3})]

    arrived(rho1_copies)
    unpack1(0, RHO1, -4, 12, -4)
    for p in range(-3, 12):
        CX1[p + 3] = coupling(RHO1[p + 3], RHO1[p + 4])
    for p in range(-3, 11):
        rho = RHO1[p + 4]
        diag = CX1[p + 3] + CX1[p + 4]
        for n, other in enumerate(shifts1(rho)):
            between = coupling(rho, other)
            C1[n, p + 3] = between
            diag = diag + between
        INV1[p + 3] = jnp.where(rho > 0.0, RELAXATION / diag, 0.0)
        if 0 <= p < 8:
            DIAG1[p] = diag

    arrived(v2_faces)
    trim0(2)
    residual = []
    for c in chunks:
        v, total = around0(2, c)
        residual += list(SRC[c:c + CHUNK] + total - DIAG0[c:c + CHUNK] * v)
    b1_copies = exchange1(1, [0.5 * t for t in down0(lambda p: residual[p])])

    arrived(rho2_x)
    for d in (-2, -1, 1, 2):
        XD[9 - 4 * d:13 - 4 * d] = jnp.where(exists("gx", -d), XD[9 - 4 * d:13 - 4 * d], 0.0)
    XD[0] = jnp.where(exists("gx", -3), XD[0], 0.0)
    XD[21] = jnp.where(exists("gx", 3), XD[21], 0.0)
    row2 = iota((20, 8, 128), 1)
    rho = XD[1:21]
    cx2 = coupling(XD[0:21], XD[1:22])
    y_up = coupling(rho, jnp.where(row2 == 7, 0.0, pltpu.roll(rho, 7, 1)))
    y_down = coupling(rho, jnp.where(row2 == 0, 0.0, pltpu.roll(rho, 1, 1)))
    z_up = coupling(rho, pltpu.roll(rho, 127, 2))
    z_down = coupling(rho, pltpu.roll(rho, 1, 2))
    diag2 = cx2[0:20] + cx2[1:21] + ((y_up + y_down) + (z_up + z_down))
    inv2 = jnp.where(rho > 0.0, RELAXATION / diag2, 0.0)
    y_up = jnp.where(row2 == 7, 0.0, y_up)
    y_down = jnp.where(row2 == 0, 0.0, y_down)

    arrived(b1_copies)
    unpack1(1, B1, -3, 11, -3)
    for p in range(-3, 11):
        W1[p + 3] = INV1[p + 3] * B1[p + 3]
    for p in range(-2, 10):
        v, total = around1(W1, p, -3)
        W2[p + 2] = KEEP * v + INV1[p + 3] * (B1[p + 3] + total)
    residual = []
    for p in range(8):
        v, total = around1(W2, p, -2)
        residual.append((B1[p + 3] + total - DIAG1[p] * v)[0:8])

    GB[2, gy] = 0.5 * down1(lambda p: residual[p])
    b2_copies = [post(GB.at[2, gy], GB.at[2 - d, gy], {"gx": d, "gy": e})
                 for d in (0, 1, -1, 2, -2) for e in (1, 2, 3, 0) if d or e]
    arrived(b2_copies)
    planes = []
    for d in (-2, -1, 0, 1, 2):
        planes += [jnp.where(exists("gx", d), t, 0.0) if d else t for t in rows_of([GB[2 + d, q] for q in range(4)])]
    b2 = jnp.stack(planes)
    v = inv2 * b2
    for k in range(1, COARSE_SWEEPS):
        z = 20 - k
        here = v[1:-1]
        total = cx2[k:z] * v[:-2] + cx2[k + 1:z + 1] * v[2:]
        total = total + y_up[k:z] * pltpu.roll(here, 7, 1) + y_down[k:z] * pltpu.roll(here, 1, 1)
        total = total + z_up[k:z] * pltpu.roll(here, 127, 2) + z_down[k:z] * pltpu.roll(here, 1, 2)
        v = KEEP * here + inv2[k:z] * (b2[k:z] + total)

    row6 = iota((6, 8, 128), 1)
    t = pltpu.roll(v, lax.rem(8 - 2 * gy, 8), 1)
    own = jnp.where(row6 < jnp.where(exists("gy", 1), 8, 4), grow(t, 1), 0.0)
    under = jnp.where(row6 >= jnp.where(exists("gy", -1), 6, 8), jnp.where(row6 == 7, t, pltpu.roll(t, 7, 1)), 0.0)
    t = dot(jnp.concatenate([own, under], axis=1).reshape(96, 128), spread1).reshape(6, 16, 256)
    for p in range(-2, 10):
        W2[p + 2] = W2[p + 2] + t[p // 2 + 1]
    for p in range(-1, 9):
        v, total = around1(W2, p, -2)
        E1[p + 1] = KEEP * v + INV1[p + 3] * (B1[p + 3] + total)

    y_low = jnp.zeros((8, 256), f32)
    y_high = y_low
    for p in range(8):
        y_low = jnp.where(row8 == p, turn(E1[p + 1, 8:16], p - 7, 0), y_low)
        y_high = jnp.where(row8 == p, turn(E1[p + 1, 0:8], p - 4, 0), y_high)
    parts = [grow(E1[p, 0:8], 0) for p in range(10)]
    for t in (y_low, y_high):
        parts += [grow(t, 0), grow(pltpu.roll(t, 4, 0), 0)]
    e = dot(jnp.concatenate(parts, axis=0), spread0)
    left(v2_faces)
    for p in range(18):
        n = (p + 1) // 2
        V0[2, p] = V0[2, p] + e[8 * n:8 * n + 8]
    YH0[2, 0] = YH0[2, 0] + e[80:96]
    YH0[2, 1] = YH0[2, 1] + e[96:112]
    for c in chunks:
        v, total = around0(2, c)
        v = KEEP * v + INV0[c:c + CHUNK] * (SRC[c:c + CHUNK] + total)
        out[c:c + CHUNK] = v[:, :, 0:256]

    done = {id(copy) for copy in to_below + to_above}
    left([copy for copy in copies if id(copy) not in sent | done])


def shards(source, phase_mask, density_factor):
    f32 = jnp.float32
    vmem = pl.BlockSpec(memory_space=pltpu.VMEM)
    shapes = [
        (3, 18, 8, 384), (16, 8, 384), (3, 2, 16, 384), (3, 2, 16, 384), (2, 16, 8, 128), (2, 16, 8, 128),
        (2, 2, 8, 128), (2, 2, 16, 128), (17, 8, 384), (4, 16, 8, 384), (16, 8, 384), (16, 8, 384),
        (2, 4, 8, 256), (2, 8, 4, 8, 256), (16, 16, 256), (15, 16, 256), (4, 14, 16, 256), (14, 16, 256), (8, 16, 256),
        (14, 16, 256), (14, 16, 256), (12, 16, 256), (10, 16, 256), (4, 8, 128), (5, 4, 8, 128), (22, 8, 128),
    ]
    return pl.pallas_call(
        kernel,
        out_shape=jax.ShapeDtypeStruct((16, 8, 256), f32),
        in_specs=[vmem] * 3,
        out_specs=vmem,
        scratch_shapes=[pltpu.VMEM(shape, f32) for shape in shapes] + [pltpu.SemaphoreType.DMA((COPIES,))] * 2,
        compiler_params=pltpu.CompilerParams(collective_id=0, has_side_effects=True),
        name="vcycle",
    )(source, phase_mask, density_factor)


def solution(mesh):
    spec = P("gx", "gy", "gz")
    return jax.shard_map(shards, mesh=mesh, in_specs=(spec,) * 3, out_specs=spec, check_vma=False)
```

time: 349 us -> 43.7 us (0.13)
  the two profiles are of different devices: /device:TPU:795 before, /device:TPU:1 now
where the time goes in v2:
time: 43.7 us; the launch traced here: 43.6 us
  Pallas kernels  42 us (96%)
  local copies, waits for them, and re-layouts  1.57 us (4%)
    pallas_call x1, Pallas kernels, shards(): pl.pallas_call(kernel, out_shape=jax.ShapeDtypeStruct((16, 8, 256), f32),...  42 us
    unnamed x1, local copies, waits for them, and re-layouts  1.57 us

profile of v2, /device:TPU:1, one launch (start us, length us, event | category | flops | bytes accessed | tf_op | source)
XLA Modules:
  0.0 43.6 jit_solution(5515030681243071807)
XLA Ops:
  0.0 42.0 %vcycle.1 = f32[16,8,256]{2,1,0:T(8,128)} custom-call(f32[16,8,256]{2,1,0:T(8,128)} %src.1, s32[16,8,256]{2,1,0:T(8,128)} %mask.1, f32[16,8,256]{2,1,0:T(8,128)} %fac.1), custom_call_target="tpu_custom_call" | custom-call | tf_op jit(solution)/shard_map/vcycle/pallas_call | solution.py:417
  42.0 1.6 %copy.5 = f32[16,8,256]{2,1,0:T(8,128)} copy(f32[16,8,256]{2,1,0:T(8,128)} %vcycle.1) | data formatting | bytes 262144

commit v3 on v2

--- a/solution.py
+++ b/solution.py
@@ -11,7 +11,7 @@
 COARSE_SWEEPS = 8
 MESH = pl.DeviceIdType.MESH
 CHUNK = 2
-COPIES = 66
+COPIES = 68
 TINY = 1e-30
 AXES = ("gx", "gy", "gz")
 SIDES = [(a, b) for a in (-1, 0, 1) for b in (-1, 0, 1) if a or b]
@@ -50,7 +50,7 @@
     return jnp.where(row < 4, low, high)
 
 
-def kernel(src, mask, fac, out, V0, SRC, YS0, YH0, ZS, ZH, HX, HY, CX0, C0, INV0, DIAG0,
+def kernel(src_in, mask_in, fac_in, out, src, mask, fac, in_sem, V0, SRC, YS0, YH0, ZS, ZH, HX, HY, CX0, C0, CB0, KB0, INV0, DIAG0, R0,
            S1, H1, RHO1, CX1, C1, INV1, DIAG1, B1, W1, W2, E1, G, GB, XD, send_sem, recv_sem):
     f32 = jnp.float32
     sizes = {axis: lax.axis_size(axis) for axis in AXES}
@@ -84,18 +84,17 @@
         for copy in group:
             copy.wait_recv()
 
-    sent = set()
-
     def left(group):
         for copy in group:
             copy.wait_send()
-            sent.add(id(copy))
+
+    inputs = [pltpu.make_async_copy(a, b, in_sem.at[n]) for n, (a, b) in enumerate(((fac_in, fac), (mask_in, mask), (src_in, src)))]
+    for copy in inputs:
+        copy.start()
 
     barrier = pltpu.get_barrier_semaphore()
-    steady = [{"gx": a, "gy": b} for a in (-2, -1, 0, 1, 2) for b in (0, 1, 2, 3) if a or b] + [{"gx": -3}, {"gx": 3}]
+    steady = [{"gx": a, "gy": b} for a in (0, -1, 1, -2, 2) for b in (0, 1, 3, 2) if a or b] + [{"gx": -3}, {"gx": 3}]
     across = [{}, {"gx": -1}, {"gx": 1}, {"gy": -1}, {"gy": 1}]
-    for way in steady:
-        pl.semaphore_signal(barrier, inc=1, device_id=peer(way), device_id_type=MESH)
     for d, there in ((-1, below), (1, above)):
         ids = [peer({**way, "gz": d}) for way in across]
 
@@ -103,10 +102,12 @@
         def _():
             for other in ids:
                 pl.semaphore_signal(barrier, inc=1, device_id=other, device_id_type=MESH)
-
-    lane16 = iota((16, 8, 128), 2)
-    row0 = iota((CHUNK, 8, 384), 1)
+    for way in steady:
+        pl.semaphore_signal(barrier, inc=1, device_id=peer(way), device_id_type=MESH)
+
+    lane16 = iota((8, 8, 128), 2)
     chunks = range(0, 16, CHUNK)
+    own, ring = slice(0, 256), slice(256, 384)
 
     def pack_y0(k, c, v):
         n = v.shape[-1]
@@ -114,52 +115,66 @@
             YS0[k, 0, c + i:c + i + 1, 0:n] = v[i, 0:1, :]
             YS0[k, 1, c + i:c + i + 1, 0:n] = v[i, 7:8, :]
 
-    def halo0(k, c):
-        return [jnp.stack([jnp.broadcast_to(YH0[k, side, c + i:c + i + 1, :], (8, 384)) for i in range(CHUNK)])
-                for side in (0, 1)]
-
-    def shifts0(v, y_low, y_high):
-        return (jnp.where(row0 == 7, y_high, pltpu.roll(v, 7, 1)), jnp.where(row0 == 0, y_low, pltpu.roll(v, 1, 1)),
-                pltpu.roll(v, 383, 2), pltpu.roll(v, 1, 2))
-
-    def around0(k, c):
+    def outer(k, c, lanes=slice(0, 384)):
+        shape = (8, lanes.stop - lanes.start)
+        first = iota(shape, 0) < 4
+        return jnp.stack([jnp.where(first, jnp.broadcast_to(YH0[k, 0, c + i:c + i + 1, lanes], shape),
+                                    jnp.broadcast_to(YH0[k, 1, c + i:c + i + 1, lanes], shape)) for i in range(CHUNK)])
+
+    def inner(k, c):
         v = V0[k, 1 + c:1 + c + CHUNK]
-        total = CX0[c:c + CHUNK] * V0[k, c:c + CHUNK] + CX0[c + 1:c + 1 + CHUNK] * V0[k, c + 2:c + 2 + CHUNK]
-        for n, other in enumerate(shifts0(v, *halo0(k, c))):
-            total = total + C0[n, c:c + CHUNK] * other
-        return v, total
+        parts = []
+        for i in range(c, c + CHUNK):
+            terms = ([CX0[i] * V0[k, i]] if i else []) + ([CX0[i + 1] * V0[k, i + 2]] if i < 15 else [])
+            parts.append(sum(terms[1:], terms[0]))
+        total = jnp.stack(parts) + C0[0, c:c + CHUNK] * pltpu.roll(v, 7, 1) + C0[1, c:c + CHUNK] * pltpu.roll(v, 1, 1)
+        return v, total + C0[2, c:c + CHUNK] * pltpu.roll(v, 383, 2) + C0[3, c:c + CHUNK] * pltpu.roll(v, 1, 2)
+
+    def ends(k, c):
+        return {i: CX0[i + (i == 15)] * V0[k, 17 if i else 0] for i in (0, 15) if c <= i < c + CHUNK}
 
     def faces0(k):
         return [post(V0.at[k, 1], V0.at[k, 17], {"gx": -1}), post(V0.at[k, 16], V0.at[k, 0], {"gx": 1}),
                 post(YS0.at[k, 0], YH0.at[k, 1], {"gy": -1}), post(YS0.at[k, 1], YH0.at[k, 0], {"gy": 1})]
 
-    def trim0(k):
-        V0[k, 0] = jnp.where(exists("gx", -1), V0[k, 0], 0.0)
-        V0[k, 17] = jnp.where(exists("gx", 1), V0[k, 17], 0.0)
-        YH0[k, 0] = jnp.where(exists("gy", -1), YH0[k, 0], 0.0)
-        YH0[k, 1] = jnp.where(exists("gy", 1), YH0[k, 1], 0.0)
-
+    def trim0(k, lanes=slice(0, 384)):
+        for side, d in ((0, -1), (1, 1)):
+            V0[k, 17 * side, :, lanes] = jnp.where(exists("gx", d), V0[k, 17 * side, :, lanes], 0.0)
+            YH0[k, side, :, lanes] = jnp.where(exists("gy", d), YH0[k, side, :, lanes], 0.0)
+
+    def pack_z0(n, field):
+        low, high = field[:, :, 0:128], field[:, :, 128:256]
+        ZS[n, 0] = jnp.where(lane16 < 64, low[0:8], pltpu.roll(low[8:16], 64, 2))
+        ZS[n, 1] = jnp.where(lane16 < 64, pltpu.roll(high[0:8], 64, 2), high[8:16])
+
+    def unpack_z0(n):
+        up, down = jnp.where(above, ZH[n, 1], 0.0), jnp.where(below, ZH[n, 0], 0.0)
+        return (jnp.where(lane16 < 64, up, pltpu.roll(down, 64, 2)), jnp.where(lane16 < 64, pltpu.roll(up, 64, 2), down))
+
+    inputs[0].wait()
+    inputs[1].wait()
     rho = jnp.where(mask[...] == 1, GAS_DENSITY, 1.0) * fac[...]
-    V0[0, 1:17, :, 0:256] = rho
-    source = src[...]
-    ZS[0] = jnp.where(lane16 < 64, rho[:, :, 0:128], pltpu.roll(source[:, :, 0:128], 64, 2))
-    ZS[1] = jnp.where(lane16 < 64, pltpu.roll(rho[:, :, 128:256], 64, 2), source[:, :, 128:256])
+    V0[0, 1:17, :, own] = rho
+    pack_z0(0, rho)
     pack_y0(0, 0, rho)
-    SRC[:, :, 0:256] = source
+    inputs[2].wait()
+    pack_z0(1, src[...])
     two = jnp.where(above, 1, 0) + jnp.where(below, 1, 0)
     pl.semaphore_wait(barrier, len(steady) + len(across) * two)
 
     low, high = pl.ds(0, 128), pl.ds(128, 128)
-    to_below = [ready(ZS.at[0], ZH.at[1], {"gz": -1}),
+    to_below = [ready(ZS.at[0, 0], ZH.at[0, 1], {"gz": -1}),
                 ready(V0.at[0, 1, :, low], HX.at[1, 1], {"gx": -1, "gz": -1}),
                 ready(V0.at[0, 16, :, low], HX.at[0, 1], {"gx": 1, "gz": -1}),
                 ready(YS0.at[0, 0, :, low], HY.at[1, 1], {"gy": -1, "gz": -1}),
-                ready(YS0.at[0, 1, :, low], HY.at[0, 1], {"gy": 1, "gz": -1})]
-    to_above = [ready(ZS.at[1], ZH.at[0], {"gz": 1}),
+                ready(YS0.at[0, 1, :, low], HY.at[0, 1], {"gy": 1, "gz": -1}),
+                ready(ZS.at[1, 0], ZH.at[1, 1], {"gz": -1})]
+    to_above = [ready(ZS.at[0, 1], ZH.at[0, 0], {"gz": 1}),
                 ready(V0.at[0, 1, :, high], HX.at[1, 0], {"gx": -1, "gz": 1}),
                 ready(V0.at[0, 16, :, high], HX.at[0, 0], {"gx": 1, "gz": 1}),
                 ready(YS0.at[0, 0, :, high], HY.at[1, 0], {"gy": -1, "gz": 1}),
-                ready(YS0.at[0, 1, :, high], HY.at[0, 0], {"gy": 1, "gz": 1})]
+                ready(YS0.at[0, 1, :, high], HY.at[0, 0], {"gy": 1, "gz": 1}),
+                ready(ZS.at[1, 1], ZH.at[1, 0], {"gz": 1})]
     for group, there in ((to_below, below), (to_above, above)):
         @pl.when(there)
         def _():
@@ -178,44 +193,79 @@
     spread0 = ones_where(a == jnp.where(b < 160, b, b + 64))
     spread1 = ones_where(iota((128, 256), 0) == lax.shift_right_logical(iota((128, 256), 1), 1))
 
+    def couple0(lanes, planes):
+        for c in planes:
+            CX0[c, :, lanes] = coupling(V0[0, c, :, lanes], V0[0, c + 1, :, lanes])
+
+    def couple0_y(lanes):
+        for c in chunks:
+            rho = V0[0, 1 + c:1 + c + CHUNK, :, lanes]
+            between = jnp.where(iota(rho.shape, 1) == 7, 0.0, coupling(rho, pltpu.roll(rho, 7, 1)))
+            C0[0, c:c + CHUNK, :, lanes] = between
+            C0[1, c:c + CHUNK, :, lanes] = pltpu.roll(between, 1, 1)
+
+    def couple0_ends(lanes):
+        for c in chunks:
+            rho = V0[0, 1 + c:1 + c + CHUNK, :, lanes]
+            row = iota(rho.shape, 1)
+            CB0[c:c + CHUNK, :, lanes] = jnp.where((row == 0) | (row == 7), coupling(rho, outer(0, c, lanes)), 0.0)
+
+    SRC[:, :, own] = src[...]
+    couple0(own, range(1, 16))
+    couple0_y(own)
     arrived(rho0_faces)
+    trim0(0, own)
+    couple0(own, (0, 16))
+    couple0_ends(own)
     for group, there in ((to_below, above), (to_above, below)):
         @pl.when(there)
         def _():
-            arrived(group)
-    for group, there in ((to_below, below), (to_above, above)):
-        @pl.when(there)
-        def _():
-            left(group)
-
-    ring = slice(256, 384)
-    up, down = jnp.where(above, ZH[1], 0.0), jnp.where(below, ZH[0], 0.0)
-    V0[0, 1:17, :, ring] = jnp.where(lane16 < 64, up, pltpu.roll(down, 64, 2))
-    SRC[:, :, ring] = jnp.where(lane16 < 64, pltpu.roll(up, 64, 2), down)
+            arrived(group[:5])
+    first, second = unpack_z0(0)
+    V0[0, 1:9, :, ring] = first
+    V0[0, 9:17, :, ring] = second
     lane8, lane2 = iota((8, 128), 1), iota((16, 128), 1)
     for side in (0, 1):
         V0[0, 17 * side, :, ring] = jnp.where(
             lane8 < 64, jnp.where(above, HX[side, 1], 0.0), jnp.where(below, HX[side, 0], 0.0))
         YH0[0, side, :, ring] = jnp.where(
             lane2 < 64, jnp.where(above, HY[side, 1], 0.0), jnp.where(below, HY[side, 0], 0.0))
-    trim0(0)
-
-    for c in range(17):
-        CX0[c] = coupling(V0[0, c], V0[0, c + 1])
-    for c in chunks:
+    trim0(0, ring)
+    couple0(ring, range(17))
+    couple0_y(ring)
+    couple0_ends(ring)
+    for c in chunks:
+        some = slice(c, c + CHUNK)
         rho = V0[0, 1 + c:1 + c + CHUNK]
-        diag = CX0[c:c + CHUNK] + CX0[c + 1:c + 1 + CHUNK]
-        for n, other in enumerate(shifts0(rho, *halo0(0, c))):
-            between = coupling(rho, other)
-            C0[n, c:c + CHUNK] = between
-            diag = diag + between
-        inv = jnp.where(rho > 0.0, RELAXATION / diag, 0.0)
-        DIAG0[c:c + CHUNK] = diag
-        INV0[c:c + CHUNK] = inv
-        v = inv * SRC[c:c + CHUNK]
+        between = coupling(rho, pltpu.roll(rho, 383, 2))
+        after = pltpu.roll(between, 1, 2)
+        C0[2, some] = between
+        C0[3, some] = after
+        diag = (CX0[some] + CX0[c + 1:c + 1 + CHUNK]) + (between + after) + (C0[0, some] + C0[1, some] + CB0[some])
+        DIAG0[some] = diag
+        INV0[some] = jnp.where(rho > 0.0, RELAXATION / diag, 0.0)
+    for group, there in ((to_below, above), (to_above, below)):
+        @pl.when(there)
+        def _():
+            arrived(group[5:])
+    first, second = unpack_z0(1)
+    SRC[0:8, :, ring] = first
+    SRC[8:16, :, ring] = second
+
+    for c in chunks:
+        v = INV0[c:c + CHUNK] * SRC[c:c + CHUNK]
         V0[1, 1 + c:1 + c + CHUNK] = v
         pack_y0(1, c, v)
     v1_faces = faces0(1)
+    for group, there in ((to_below, below), (to_above, above)):
+        @pl.when(there)
+        def _():
+            left(group)
+    for c in chunks:
+        some = slice(c, c + CHUNK)
+        v, total = inner(1, c)
+        V0[2, 1 + c:1 + c + CHUNK] = KEEP * v + INV0[some] * (SRC[some] + total)
+        KB0[some] = INV0[some] * CB0[some]
 
     row8 = iota((8, 256), 0)
     row8s = iota((8, 128), 0)
@@ -237,6 +287,8 @@
         group = []
         for a, b in ((1, 0), (-1, 0), (0, 1), (0, -1), (1, 1), (1, -1), (-1, 1), (-1, -1)):
             some = {1: pl.ds(2, 2), -1: pl.ds(0, 2), 0: pl.ds(0, 4)}[a]
+            if k and a and b:
+                some = pl.ds(3 if a > 0 else 0, 1)
             group.append(post(S1.at[k, some], H1.at[k, slot(-a, -b), some], {"gx": a, "gy": b}))
         return group
 
@@ -248,6 +300,8 @@
             def block(b):
                 if not a and not b:
                     return S1[k, j]
+                if k and a and b and j in (1, 2):
+                    return jnp.zeros((8, 256), f32)
                 return jnp.where(exists("gx", a) & exists("gy", b), H1[k, slot(a, b), j], 0.0)
 
             target[p - offset, 0:8] = jnp.where(row8 < 4, turn(block(0), -4 * half, 0), turn(block(1), 4 - 4 * half, 0))
@@ -280,11 +334,15 @@
     arrived(v1_faces)
     trim0(1)
     for c in chunks:
-        v, total = around0(1, c)
-        v = KEEP * v + INV0[c:c + CHUNK] * (SRC[c:c + CHUNK] + total)
+        for i, term in ends(1, c).items():
+            V0[2, 1 + i] = V0[2, 1 + i] + INV0[i] * term
+        v = V0[2, 1 + c:1 + c + CHUNK] + KB0[c:c + CHUNK] * outer(1, c)
         V0[2, 1 + c:1 + c + CHUNK] = v
         pack_y0(2, c, v)
     v2_faces = faces0(2)
+    for c in chunks:
+        v, total = inner(2, c)
+        R0[c:c + CHUNK] = SRC[c:c + CHUNK] + total - DIAG0[c:c + CHUNK] * v
 
     def rows_of(blocks):
         planes = []
@@ -320,8 +378,9 @@
     trim0(2)
     residual = []
     for c in chunks:
-        v, total = around0(2, c)
-        residual += list(SRC[c:c + CHUNK] + total - DIAG0[c:c + CHUNK] * v)
+        r = R0[c:c + CHUNK] + CB0[c:c + CHUNK] * outer(2, c)
+        more = ends(2, c)
+        residual += [r[i] + more[c + i] if c + i in more else r[i] for i in range(CHUNK)]
     b1_copies = exchange1(1, [0.5 * t for t in down0(lambda p: residual[p])])
 
     arrived(rho2_x)
@@ -355,7 +414,9 @@
 
     GB[2, gy] = 0.5 * down1(lambda p: residual[p])
     b2_copies = [post(GB.at[2, gy], GB.at[2 - d, gy], {"gx": d, "gy": e})
-                 for d in (0, 1, -1, 2, -2) for e in (1, 2, 3, 0) if d or e]
+                 for e in (2, 1, 3, 0) for d in (2, -2, 1, -1, 0) if d or e]
+    late = {id(copy) for copy in b2_copies + to_below + to_above}
+    left([copy for copy in copies if id(copy) not in late])
     arrived(b2_copies)
     planes = []
     for d in (-2, -1, 0, 1, 2):
@@ -372,9 +433,9 @@
 
     row6 = iota((6, 8, 128), 1)
     t = pltpu.roll(v, lax.rem(8 - 2 * gy, 8), 1)
-    own = jnp.where(row6 < jnp.where(exists("gy", 1), 8, 4), grow(t, 1), 0.0)
+    over = jnp.where(row6 < jnp.where(exists("gy", 1), 8, 4), grow(t, 1), 0.0)
     under = jnp.where(row6 >= jnp.where(exists("gy", -1), 6, 8), jnp.where(row6 == 7, t, pltpu.roll(t, 7, 1)), 0.0)
-    t = dot(jnp.concatenate([own, under], axis=1).reshape(96, 128), spread1).reshape(6, 16, 256)
+    t = dot(jnp.concatenate([over, under], axis=1).reshape(96, 128), spread1).reshape(6, 16, 256)
     for p in range(-2, 10):
         W2[p + 2] = W2[p + 2] + t[p // 2 + 1]
     for p in range(-1, 9):
@@ -390,36 +451,38 @@
     for t in (y_low, y_high):
         parts += [grow(t, 0), grow(pltpu.roll(t, 4, 0), 0)]
     e = dot(jnp.concatenate(parts, axis=0), spread0)
-    left(v2_faces)
     for p in range(18):
         n = (p + 1) // 2
         V0[2, p] = V0[2, p] + e[8 * n:8 * n + 8]
     YH0[2, 0] = YH0[2, 0] + e[80:96]
     YH0[2, 1] = YH0[2, 1] + e[96:112]
     for c in chunks:
-        v, total = around0(2, c)
+        v, total = inner(2, c)
+        more = ends(2, c)
+        total = total + CB0[c:c + CHUNK] * outer(2, c)
+        total = jnp.stack([total[i] + more[c + i] if c + i in more else total[i] for i in range(CHUNK)])
         v = KEEP * v + INV0[c:c + CHUNK] * (SRC[c:c + CHUNK] + total)
-        out[c:c + CHUNK] = v[:, :, 0:256]
-
-    done = {id(copy) for copy in to_below + to_above}
-    left([copy for copy in copies if id(copy) not in sent | done])
+        out[c:c + CHUNK] = v[:, :, own]
+
+    left(b2_copies)
 
 
 def shards(source, phase_mask, density_factor):
     f32 = jnp.float32
-    vmem = pl.BlockSpec(memory_space=pltpu.VMEM)
     shapes = [
-        (3, 18, 8, 384), (16, 8, 384), (3, 2, 16, 384), (3, 2, 16, 384), (2, 16, 8, 128), (2, 16, 8, 128),
+        (3, 18, 8, 384), (16, 8, 384), (3, 2, 16, 384), (3, 2, 16, 384), (2, 2, 8, 8, 128), (2, 2, 8, 8, 128),
         (2, 2, 8, 128), (2, 2, 16, 128), (17, 8, 384), (4, 16, 8, 384), (16, 8, 384), (16, 8, 384),
+        (16, 8, 384), (16, 8, 384), (16, 8, 384),
         (2, 4, 8, 256), (2, 8, 4, 8, 256), (16, 16, 256), (15, 16, 256), (4, 14, 16, 256), (14, 16, 256), (8, 16, 256),
         (14, 16, 256), (14, 16, 256), (12, 16, 256), (10, 16, 256), (4, 8, 128), (5, 4, 8, 128), (22, 8, 128),
     ]
     return pl.pallas_call(
         kernel,
-        out_shape=jax.ShapeDtypeStruct((16, 8, 256), f32),
-        in_specs=[vmem] * 3,
-        out_specs=vmem,
-        scratch_shapes=[pltpu.VMEM(shape, f32) for shape in shapes] + [pltpu.SemaphoreType.DMA((COPIES,))] * 2,
+        out_shape=pltpu.VMEM((16, 8, 256), f32),
+        in_specs=[pl.BlockSpec(memory_space=pl.ANY)] * 3,
+        out_specs=pl.BlockSpec(memory_space=pltpu.VMEM),
+        scratch_shapes=[pltpu.VMEM((16, 8, 256), kind) for kind in (f32, jnp.int32, f32)] + [pltpu.SemaphoreType.DMA((3,))]
+        + [pltpu.VMEM(shape, f32) for shape in shapes] + [pltpu.SemaphoreType.DMA((COPIES,))] * 2,
         compiler_params=pltpu.CompilerParams(collective_id=0, has_side_effects=True),
         name="vcycle",
     )(source, phase_mask, density_factor)

time: 43.7 us -> 40 us (0.915)
  Pallas kernels: 42 us -> 39.2 us
  local copies, waits for them, and re-layouts: 1.57 us -> 0.66 us
    pallas_call x1, Pallas kernels: 42 us -> 39.2 us  [shards(): pl.pallas_call(kernel, out_shape=pltpu.VMEM((16, 8, 256), f32), in_specs=...]
    unnamed x1, local copies, waits for them, and re-layouts: 1.57 us -> 0.66 us
where the time goes in v3:
time: 40 us; the launch traced here: 39.9 us
  Pallas kernels  39.2 us (98%)
  local copies, waits for them, and re-layouts  0.66 us (2%)
    pallas_call x1, Pallas kernels, shards(): pl.pallas_call(kernel, out_shape=pltpu.VMEM((16, 8, 256), f32), in_specs=...  39.2 us

profile of v3, /device:TPU:1, one launch (start us, length us, event | category | flops | bytes accessed | tf_op | source)
XLA Modules:
  0.0 39.9 jit_solution(7665639161205904234)
XLA Ops:
  0.0 39.2 %vcycle.1 = f32[16,8,256]{2,1,0:T(8,128)S(1)} custom-call(f32[16,8,256]{2,1,0:T(8,128)} %src_in.1, s32[16,8,256]{2,1,0:T(8,128)} %mask_in.1, f32[16,8,256]{2,1,0:T(8,128)} %fac_in.1), custom_call_target="tpu_custom_call" | custom-call | tf_op jit(solution)/shard_map/vcycle/pallas_call | solution.py:479
  39.2 0.7 %copy.5 = f32[16,8,256]{2,1,0:T(8,128)} copy(f32[16,8,256]{2,1,0:T(8,128)S(1)} %vcycle.1) | data formatting | bytes 262144

commit v4 on v3

--- a/solution.py
+++ b/solution.py
@@ -134,8 +134,8 @@
         return {i: CX0[i + (i == 15)] * V0[k, 17 if i else 0] for i in (0, 15) if c <= i < c + CHUNK}
 
     def faces0(k):
-        return [post(V0.at[k, 1], V0.at[k, 17], {"gx": -1}), post(V0.at[k, 16], V0.at[k, 0], {"gx": 1}),
-                post(YS0.at[k, 0], YH0.at[k, 1], {"gy": -1}), post(YS0.at[k, 1], YH0.at[k, 0], {"gy": 1})]
+        return [post(YS0.at[k, 0], YH0.at[k, 1], {"gy": -1}), post(YS0.at[k, 1], YH0.at[k, 0], {"gy": 1}),
+                post(V0.at[k, 1], V0.at[k, 17], {"gx": -1}), post(V0.at[k, 16], V0.at[k, 0], {"gx": 1})]
 
     def trim0(k, lanes=slice(0, 384)):
         for side, d in ((0, -1), (1, 1)):
@@ -175,16 +175,21 @@
                 ready(YS0.at[0, 0, :, high], HY.at[1, 0], {"gy": -1, "gz": 1}),
                 ready(YS0.at[0, 1, :, high], HY.at[0, 0], {"gy": 1, "gz": 1}),
                 ready(ZS.at[1, 1], ZH.at[1, 0], {"gz": 1})]
-    for group, there in ((to_below, below), (to_above, above)):
-        @pl.when(there)
-        def _():
-            for copy in group:
-                copy.start()
+    for some in (slice(1, 5), slice(0, 1)):
+        for group, there in ((to_below, below), (to_above, above)):
+            @pl.when(there)
+            def _():
+                for copy in group[some]:
+                    copy.start()
     both = pl.ds(0, 256)
     rho0_faces = [post(V0.at[0, 1, :, both], V0.at[0, 17, :, both], {"gx": -1}),
                   post(V0.at[0, 16, :, both], V0.at[0, 0, :, both], {"gx": 1}),
                   post(YS0.at[0, 0, :, both], YH0.at[0, 1, :, both], {"gy": -1}),
                   post(YS0.at[0, 1, :, both], YH0.at[0, 0, :, both], {"gy": 1})]
+    for group, there in ((to_below, below), (to_above, above)):
+        @pl.when(there)
+        def _():
+            group[5].start()
 
     a, b = lax.shift_right_logical(iota((384, 256), 0), 1), iota((384, 256), 1)
     pairs0 = ones_where(b == jnp.where(a < 160, a, a + 64))
@@ -213,6 +218,11 @@
     SRC[:, :, own] = src[...]
     couple0(own, range(1, 16))
     couple0_y(own)
+    for c in chunks:
+        rho = V0[0, 1 + c:1 + c + CHUNK, :, own]
+        between = coupling(rho, pltpu.roll(rho, 255, 2))
+        C0[2, c:c + CHUNK, :, own] = between
+        C0[3, c:c + CHUNK, :, own] = pltpu.roll(between, 1, 2)
     arrived(rho0_faces)
     trim0(0, own)
     couple0(own, (0, 16))
@@ -237,10 +247,16 @@
     for c in chunks:
         some = slice(c, c + CHUNK)
         rho = V0[0, 1 + c:1 + c + CHUNK]
-        between = coupling(rho, pltpu.roll(rho, 383, 2))
-        after = pltpu.roll(between, 1, 2)
-        C0[2, some] = between
-        C0[3, some] = after
+        outside = rho[:, :, ring]
+        lane = iota(outside.shape, 2)
+        up = jnp.where(lane == 127, pltpu.roll(rho[:, :, 0:128], 127, 2), pltpu.roll(outside, 127, 2))
+        down = jnp.where(lane == 0, pltpu.roll(rho[:, :, 128:256], 1, 2), pltpu.roll(outside, 1, 2))
+        up, down = coupling(outside, up), coupling(outside, down)
+        C0[2, some, :, ring] = up
+        C0[3, some, :, ring] = down
+        C0[2, some, :, 128:256] = jnp.where(lane == 127, pltpu.roll(down, 127, 2), C0[2, some, :, 128:256])
+        C0[3, some, :, 0:128] = jnp.where(lane == 0, pltpu.roll(up, 1, 2), C0[3, some, :, 0:128])
+        between, after = C0[2, some], C0[3, some]
         diag = (CX0[some] + CX0[c + 1:c + 1 + CHUNK]) + (between + after) + (C0[0, some] + C0[1, some] + CB0[some])
         DIAG0[some] = diag
         INV0[some] = jnp.where(rho > 0.0, RELAXATION / diag, 0.0)
@@ -270,13 +286,20 @@
     row8 = iota((8, 256), 0)
     row8s = iota((8, 128), 0)
 
+    row24 = iota((8, 384), 0)
+
     def down0(plane):
-        t = jnp.concatenate([plane(2 * p) + plane(2 * p + 1) for p in range(8)], axis=0)
-        t = dot(t, pairs0).reshape(8, 8, 256)
-        t = t + pltpu.roll(t, 7, 1)
-        row = iota((8, 8, 256), 1)
-        t = jnp.where(row < 1, t, jnp.where(row < 2, pltpu.roll(t, 7, 1), jnp.where(row < 3, pltpu.roll(t, 6, 1), pltpu.roll(t, 5, 1))))
-        return [jnp.where(row8 < 4, t[2 * j], pltpu.roll(t[2 * j + 1], 4, 0)) for j in range(4)]
+        tiles = []
+        for j in range(4):
+            t, u = (plane(4 * j + n) + plane(4 * j + n + 1) for n in (0, 2))
+            t, u = (x + pltpu.roll(x, 7, 0) for x in (t, u))
+            tile = pltpu.roll(u, 1, 0)
+            for n, part in ((7, pltpu.roll(u, 2, 0)), (6, pltpu.roll(u, 3, 0)), (5, pltpu.roll(u, 4, 0)),
+                            (4, pltpu.roll(t, 5, 0)), (3, pltpu.roll(t, 6, 0)), (2, pltpu.roll(t, 7, 0)), (1, t)):
+                tile = jnp.where(row24 < n, part, tile)
+            tiles.append(tile)
+        t = dot(jnp.concatenate(tiles, axis=0), pairs0)
+        return [t[8 * j:8 * j + 8] for j in range(4)]
 
     def slot(a, b):
         return SIDES.index((a, b))
@@ -285,7 +308,7 @@
         for j in range(4):
             S1[k, j] = packed[j]
         group = []
-        for a, b in ((1, 0), (-1, 0), (0, 1), (0, -1), (1, 1), (1, -1), (-1, 1), (-1, -1)):
+        for a, b in ((1, 1), (1, -1), (-1, 1), (-1, -1), (0, 1), (0, -1), (1, 0), (-1, 0)):
             some = {1: pl.ds(2, 2), -1: pl.ds(0, 2), 0: pl.ds(0, 4)}[a]
             if k and a and b:
                 some = pl.ds(3 if a > 0 else 0, 1)
@@ -404,17 +427,27 @@
     unpack1(1, B1, -3, 11, -3)
     for p in range(-3, 11):
         W1[p + 3] = INV1[p + 3] * B1[p + 3]
-    for p in range(-2, 10):
+    near, far = slice(0, 8), slice(8, 16)
+
+    def second1(p, rows):
         v, total = around1(W1, p, -3)
-        W2[p + 2] = KEEP * v + INV1[p + 3] * (B1[p + 3] + total)
+        for some in rows:
+            W2[p + 2, some] = (KEEP * v + INV1[p + 3] * (B1[p + 3] + total))[some]
+
+    for p in range(-1, 9):
+        second1(p, (near, far) if 0 <= p < 8 else (near,))
     residual = []
     for p in range(8):
         v, total = around1(W2, p, -2)
-        residual.append((B1[p + 3] + total - DIAG1[p] * v)[0:8])
+        residual.append((B1[p + 3] + total - DIAG1[p] * v)[near])
 
     GB[2, gy] = 0.5 * down1(lambda p: residual[p])
     b2_copies = [post(GB.at[2, gy], GB.at[2 - d, gy], {"gx": d, "gy": e})
                  for e in (2, 1, 3, 0) for d in (2, -2, 1, -1, 0) if d or e]
+    second1(-2, (near,))
+    second1(-1, (far,))
+    second1(8, (far,))
+    second1(9, (near,))
     late = {id(copy) for copy in b2_copies + to_below + to_above}
     left([copy for copy in copies if id(copy) not in late])
     arrived(b2_copies)
@@ -437,10 +470,14 @@
     under = jnp.where(row6 >= jnp.where(exists("gy", -1), 6, 8), jnp.where(row6 == 7, t, pltpu.roll(t, 7, 1)), 0.0)
     t = dot(jnp.concatenate([over, under], axis=1).reshape(96, 128), spread1).reshape(6, 16, 256)
     for p in range(-2, 10):
-        W2[p + 2] = W2[p + 2] + t[p // 2 + 1]
+        for some in (near, far) if -2 < p < 9 else (near,):
+            W2[p + 2, some] = W2[p + 2, some] + t[p // 2 + 1, some]
     for p in range(-1, 9):
         v, total = around1(W2, p, -2)
-        E1[p + 1] = KEEP * v + INV1[p + 3] * (B1[p + 3] + total)
+        v = KEEP * v + INV1[p + 3] * (B1[p + 3] + total)
+        E1[p + 1, near] = v[near]
+        if 0 <= p < 8:
+            E1[p + 1, far] = v[far]
 
     y_low = jnp.zeros((8, 256), f32)
     y_high = y_low

time: 40 us -> 39.5 us (0.988)
  Pallas kernels: 39.2 us -> 38.6 us
    pallas_call x1, Pallas kernels: 39.2 us -> 38.6 us  [shards(): pl.pallas_call(kernel, out_shape=pltpu.VMEM((16, 8, 256), f32), in_specs=...]
where the time goes in v4:
time: 39.5 us; the launch traced here: 39.3 us
  Pallas kernels  38.6 us (98%)
  local copies, waits for them, and re-layouts  0.66 us (2%)
    pallas_call x1, Pallas kernels, shards(): pl.pallas_call(kernel, out_shape=pltpu.VMEM((16, 8, 256), f32), in_specs=...  38.6 us

profile of v4, /device:TPU:1, one launch (start us, length us, event | category | flops | bytes accessed | tf_op | source)
XLA Modules:
  0.0 39.3 jit_solution(2290566182242269051)
XLA Ops:
  0.0 38.6 %vcycle.1 = f32[16,8,256]{2,1,0:T(8,128)S(1)} custom-call(f32[16,8,256]{2,1,0:T(8,128)} %src_in.1, s32[16,8,256]{2,1,0:T(8,128)} %mask_in.1, f32[16,8,256]{2,1,0:T(8,128)} %fac_in.1), custom_call_target="tpu_custom_call" | custom-call | tf_op jit(solution)/shard_map/vcycle/pallas_call | solution.py:516
  38.6 0.7 %copy.5 = f32[16,8,256]{2,1,0:T(8,128)} copy(f32[16,8,256]{2,1,0:T(8,128)S(1)} %vcycle.1) | data formatting | bytes 262144

commit v5 on v4

--- a/solution.py
+++ b/solution.py
@@ -444,10 +444,24 @@
     GB[2, gy] = 0.5 * down1(lambda p: residual[p])
     b2_copies = [post(GB.at[2, gy], GB.at[2 - d, gy], {"gx": d, "gy": e})
                  for e in (2, 1, 3, 0) for d in (2, -2, 1, -1, 0) if d or e]
-    second1(-2, (near,))
-    second1(-1, (far,))
-    second1(8, (far,))
-    second1(9, (near,))
+    @pl.when(gx >= 0)
+    def _():
+        second1(-2, (near,))
+        second1(-1, (far,))
+        second1(8, (far,))
+        second1(9, (near,))
+        for p in range(-1, 9):
+            v, total = around1(W2, p, -2)
+            v = KEEP * v + INV1[p + 3] * (B1[p + 3] + total)
+            for some in (near, far) if 0 <= p < 8 else (near,):
+                E1[p + 1, some] = v[some]
+        for c in chunks:
+            v, total = inner(2, c)
+            more = ends(2, c)
+            total = total + CB0[c:c + CHUNK] * outer(2, c)
+            total = jnp.stack([total[i] + more[c + i] if c + i in more else total[i] for i in range(CHUNK)])
+            v = KEEP * v + INV0[c:c + CHUNK] * (SRC[c:c + CHUNK] + total)
+            out[c:c + CHUNK] = v[:, :, own]
     late = {id(copy) for copy in b2_copies + to_below + to_above}
     left([copy for copy in copies if id(copy) not in late])
     arrived(b2_copies)
@@ -469,37 +483,33 @@
     over = jnp.where(row6 < jnp.where(exists("gy", 1), 8, 4), grow(t, 1), 0.0)
     under = jnp.where(row6 >= jnp.where(exists("gy", -1), 6, 8), jnp.where(row6 == 7, t, pltpu.roll(t, 7, 1)), 0.0)
     t = dot(jnp.concatenate([over, under], axis=1).reshape(96, 128), spread1).reshape(6, 16, 256)
-    for p in range(-2, 10):
-        for some in (near, far) if -2 < p < 9 else (near,):
-            W2[p + 2, some] = W2[p + 2, some] + t[p // 2 + 1, some]
+    moved = [shifts1(t[j]) for j in range(6)]
     for p in range(-1, 9):
-        v, total = around1(W2, p, -2)
-        v = KEEP * v + INV1[p + 3] * (B1[p + 3] + total)
-        E1[p + 1, near] = v[near]
-        if 0 <= p < 8:
-            E1[p + 1, far] = v[far]
+        j = p // 2 + 1
+        total = CX1[p + 3] * t[(p - 1) // 2 + 1] + CX1[p + 4] * t[(p + 1) // 2 + 1]
+        for n, other in enumerate(moved[j]):
+            total = total + C1[n, p + 3] * other
+        v = E1[p + 1] + (KEEP * t[j] + INV1[p + 3] * total)
+        for some in (near, far) if 0 <= p < 8 else (near,):
+            E1[p + 1, some] = v[some]
 
     y_low = jnp.zeros((8, 256), f32)
     y_high = y_low
     for p in range(8):
-        y_low = jnp.where(row8 == p, turn(E1[p + 1, 8:16], p - 7, 0), y_low)
-        y_high = jnp.where(row8 == p, turn(E1[p + 1, 0:8], p - 4, 0), y_high)
-    parts = [grow(E1[p, 0:8], 0) for p in range(10)]
-    for t in (y_low, y_high):
-        parts += [grow(t, 0), grow(pltpu.roll(t, 4, 0), 0)]
-    e = dot(jnp.concatenate(parts, axis=0), spread0)
-    for p in range(18):
-        n = (p + 1) // 2
-        V0[2, p] = V0[2, p] + e[8 * n:8 * n + 8]
-    YH0[2, 0] = YH0[2, 0] + e[80:96]
-    YH0[2, 1] = YH0[2, 1] + e[96:112]
-    for c in chunks:
-        v, total = inner(2, c)
-        more = ends(2, c)
-        total = total + CB0[c:c + CHUNK] * outer(2, c)
-        total = jnp.stack([total[i] + more[c + i] if c + i in more else total[i] for i in range(CHUNK)])
-        v = KEEP * v + INV0[c:c + CHUNK] * (SRC[c:c + CHUNK] + total)
-        out[c:c + CHUNK] = v[:, :, own]
+        y_low = jnp.where(row8 == p, turn(E1[p + 1, far], p - 7, 0), y_low)
+        y_high = jnp.where(row8 == p, turn(E1[p + 1, near], p - 4, 0), y_high)
+    e = dot(jnp.concatenate([grow(E1[p, near], 0) for p in range(10)] + [y_low, y_high], axis=0), spread0)
+    for m in range(8):
+        here = e[8 * m + 8:8 * m + 16]
+        beside = [x[:, own] for x in (pltpu.roll(here, 7, 0), pltpu.roll(here, 1, 0), pltpu.roll(here, 383, 1), pltpu.roll(here, 1, 1))]
+        outside = jnp.where(row8 < 4, jnp.broadcast_to(e[80 + m:81 + m, own], (8, 256)), jnp.broadcast_to(e[88 + m:89 + m, own], (8, 256)))
+        here = here[:, own]
+        ways = ((e[8 * m:8 * m + 8, own], here), (here, e[8 * m + 16:8 * m + 24, own]))
+        for i, (under, over) in zip((2 * m, 2 * m + 1), ways):
+            total = CX0[i, :, own] * under + CX0[i + 1, :, own] * over + CB0[i, :, own] * outside
+            for n in range(4):
+                total = total + C0[n, i, :, own] * beside[n]
+            out[i] = out[i] + (KEEP * here + INV0[i, :, own] * total)
 
     left(b2_copies)
 

time: 39.5 us -> 39.3 us (level)
  no operation moved by 1% of the time
where the time goes in v5:
time: 39.3 us; the launch traced here: 39.2 us
  Pallas kernels  38.5 us (98%)
  local copies, waits for them, and re-layouts  0.66 us (2%)
    pallas_call x1, Pallas kernels, shards(): pl.pallas_call(kernel, out_shape=pltpu.VMEM((16, 8, 256), f32), in_specs=...  38.5 us

profile of v5, /device:TPU:1, one launch (start us, length us, event | category | flops | bytes accessed | tf_op | source)
XLA Modules:
  0.0 39.2 jit_solution(390115718689922389)
XLA Ops:
  0.0 38.5 %vcycle.1 = f32[16,8,256]{2,1,0:T(8,128)S(1)} custom-call(f32[16,8,256]{2,1,0:T(8,128)} %src_in.1, s32[16,8,256]{2,1,0:T(8,128)} %mask_in.1, f32[16,8,256]{2,1,0:T(8,128)} %fac_in.1), custom_call_target="tpu_custom_call" | custom-call | tf_op jit(solution)/shard_map/vcycle/pallas_call | solution.py:526
  38.5 0.7 %copy.5 = f32[16,8,256]{2,1,0:T(8,128)} copy(f32[16,8,256]{2,1,0:T(8,128)S(1)} %vcycle.1) | data formatting | bytes 262144

commit v6 on v5

--- a/solution.py
+++ b/solution.py
@@ -227,23 +227,26 @@
     trim0(0, own)
     couple0(own, (0, 16))
     couple0_ends(own)
-    for group, there in ((to_below, above), (to_above, below)):
-        @pl.when(there)
-        def _():
-            arrived(group[:5])
+    def await_z(some):
+        for group, there in ((to_below, above), (to_above, below)):
+            @pl.when(there)
+            def _():
+                arrived(group[some])
+
+    def invert0(lanes):
+        for c in chunks:
+            some = slice(c, c + CHUNK)
+            diag = ((CX0[some, :, lanes] + CX0[c + 1:c + 1 + CHUNK, :, lanes]) + (C0[2, some, :, lanes] + C0[3, some, :, lanes])
+                    + (C0[0, some, :, lanes] + C0[1, some, :, lanes] + CB0[some, :, lanes]))
+            DIAG0[some, :, lanes] = diag
+            INV0[some, :, lanes] = jnp.where(V0[0, 1 + c:1 + c + CHUNK, :, lanes] > 0.0, RELAXATION / diag, 0.0)
+
+    await_z(slice(0, 1))
     first, second = unpack_z0(0)
     V0[0, 1:9, :, ring] = first
     V0[0, 9:17, :, ring] = second
-    lane8, lane2 = iota((8, 128), 1), iota((16, 128), 1)
-    for side in (0, 1):
-        V0[0, 17 * side, :, ring] = jnp.where(
-            lane8 < 64, jnp.where(above, HX[side, 1], 0.0), jnp.where(below, HX[side, 0], 0.0))
-        YH0[0, side, :, ring] = jnp.where(
-            lane2 < 64, jnp.where(above, HY[side, 1], 0.0), jnp.where(below, HY[side, 0], 0.0))
-    trim0(0, ring)
-    couple0(ring, range(17))
+    couple0(ring, range(1, 16))
     couple0_y(ring)
-    couple0_ends(ring)
     for c in chunks:
         some = slice(c, c + CHUNK)
         rho = V0[0, 1 + c:1 + c + CHUNK]
@@ -256,14 +259,19 @@
         C0[3, some, :, ring] = down
         C0[2, some, :, 128:256] = jnp.where(lane == 127, pltpu.roll(down, 127, 2), C0[2, some, :, 128:256])
         C0[3, some, :, 0:128] = jnp.where(lane == 0, pltpu.roll(up, 1, 2), C0[3, some, :, 0:128])
-        between, after = C0[2, some], C0[3, some]
-        diag = (CX0[some] + CX0[c + 1:c + 1 + CHUNK]) + (between + after) + (C0[0, some] + C0[1, some] + CB0[some])
-        DIAG0[some] = diag
-        INV0[some] = jnp.where(rho > 0.0, RELAXATION / diag, 0.0)
-    for group, there in ((to_below, above), (to_above, below)):
-        @pl.when(there)
-        def _():
-            arrived(group[5:])
+    invert0(own)
+    await_z(slice(1, 5))
+    lane8, lane2 = iota((8, 128), 1), iota((16, 128), 1)
+    for side in (0, 1):
+        V0[0, 17 * side, :, ring] = jnp.where(
+            lane8 < 64, jnp.where(above, HX[side, 1], 0.0), jnp.where(below, HX[side, 0], 0.0))
+        YH0[0, side, :, ring] = jnp.where(
+            lane2 < 64, jnp.where(above, HY[side, 1], 0.0), jnp.where(below, HY[side, 0], 0.0))
+    trim0(0, ring)
+    couple0(ring, (0, 16))
+    couple0_ends(ring)
+    invert0(ring)
+    await_z(slice(5, 6))
     first, second = unpack_z0(1)
     SRC[0:8, :, ring] = first
     SRC[8:16, :, ring] = second
@@ -420,8 +428,10 @@
     z_down = coupling(rho, pltpu.roll(rho, 1, 2))
     diag2 = cx2[0:20] + cx2[1:21] + ((y_up + y_down) + (z_up + z_down))
     inv2 = jnp.where(rho > 0.0, RELAXATION / diag2, 0.0)
-    y_up = jnp.where(row2 == 7, 0.0, y_up)
-    y_down = jnp.where(row2 == 0, 0.0, y_down)
+    x_low, x_high = inv2 * cx2[0:20], inv2 * cx2[1:21]
+    y_up = jnp.where(row2 == 7, 0.0, inv2 * y_up)
+    y_down = jnp.where(row2 == 0, 0.0, inv2 * y_down)
+    z_up, z_down = inv2 * z_up, inv2 * z_down
 
     arrived(b1_copies)
     unpack1(1, B1, -3, 11, -3)
@@ -462,21 +472,21 @@
             total = jnp.stack([total[i] + more[c + i] if c + i in more else total[i] for i in range(CHUNK)])
             v = KEEP * v + INV0[c:c + CHUNK] * (SRC[c:c + CHUNK] + total)
             out[c:c + CHUNK] = v[:, :, own]
-    late = {id(copy) for copy in b2_copies + to_below + to_above}
+    late = {id(copy) for copy in to_below + to_above}
     left([copy for copy in copies if id(copy) not in late])
     arrived(b2_copies)
     planes = []
     for d in (-2, -1, 0, 1, 2):
         planes += [jnp.where(exists("gx", d), t, 0.0) if d else t for t in rows_of([GB[2 + d, q] for q in range(4)])]
-    b2 = jnp.stack(planes)
-    v = inv2 * b2
+    start = inv2 * jnp.stack(planes)
+    v = start
     for k in range(1, COARSE_SWEEPS):
         z = 20 - k
         here = v[1:-1]
-        total = cx2[k:z] * v[:-2] + cx2[k + 1:z + 1] * v[2:]
+        total = x_low[k:z] * v[:-2] + x_high[k:z] * v[2:]
         total = total + y_up[k:z] * pltpu.roll(here, 7, 1) + y_down[k:z] * pltpu.roll(here, 1, 1)
         total = total + z_up[k:z] * pltpu.roll(here, 127, 2) + z_down[k:z] * pltpu.roll(here, 1, 2)
-        v = KEEP * here + inv2[k:z] * (b2[k:z] + total)
+        v = (KEEP * here + start[k:z]) + total
 
     row6 = iota((6, 8, 128), 1)
     t = pltpu.roll(v, lax.rem(8 - 2 * gy, 8), 1)
@@ -510,8 +520,6 @@
             for n in range(4):
                 total = total + C0[n, i, :, own] * beside[n]
             out[i] = out[i] + (KEEP * here + INV0[i, :, own] * total)
-
-    left(b2_copies)
 
 
 def shards(source, phase_mask, density_factor):

time: 39.3 us -> 39.2 us (level)
  no operation moved by 1% of the time
where the time goes in v6:
time: 39.2 us; the launch traced here: 39 us
  Pallas kernels  38.4 us (98%)
  local copies, waits for them, and re-layouts  0.66 us (2%)
    pallas_call x1, Pallas kernels, shards(): pl.pallas_call(kernel, out_shape=pltpu.VMEM((16, 8, 256), f32), in_specs=...  38.4 us

profile of v6, /device:TPU:1, one launch (start us, length us, event | category | flops | bytes accessed | tf_op | source)
XLA Modules:
  0.0 39.0 jit_solution(11108531379243685949)
XLA Ops:
  0.0 38.4 %vcycle.1 = f32[16,8,256]{2,1,0:T(8,128)S(1)} custom-call(f32[16,8,256]{2,1,0:T(8,128)} %src_in.1, s32[16,8,256]{2,1,0:T(8,128)} %mask_in.1, f32[16,8,256]{2,1,0:T(8,128)} %fac_in.1), custom_call_target="tpu_custom_call" | custom-call | tf_op jit(solution)/shard_map/vcycle/pallas_call | solution.py:534
  38.4 0.7 %copy.5 = f32[16,8,256]{2,1,0:T(8,128)} copy(f32[16,8,256]{2,1,0:T(8,128)S(1)} %vcycle.1) | data formatting | bytes 262144

commit v7 on v6

--- a/solution.py
+++ b/solution.py
@@ -433,23 +433,37 @@
     y_down = jnp.where(row2 == 0, 0.0, inv2 * y_down)
     z_up, z_down = inv2 * z_up, inv2 * z_down
 
-    arrived(b1_copies)
-    unpack1(1, B1, -3, 11, -3)
-    for p in range(-3, 11):
-        W1[p + 3] = INV1[p + 3] * B1[p + 3]
     near, far = slice(0, 8), slice(8, 16)
+
+    def first1(planes):
+        for p in planes:
+            W1[p + 3] = INV1[p + 3] * B1[p + 3]
 
     def second1(p, rows):
         v, total = around1(W1, p, -3)
         for some in rows:
             W2[p + 2, some] = (KEEP * v + INV1[p + 3] * (B1[p + 3] + total))[some]
 
-    for p in range(-1, 9):
-        second1(p, (near, far) if 0 <= p < 8 else (near,))
-    residual = []
-    for p in range(8):
+    def residual1(p):
         v, total = around1(W2, p, -2)
-        residual.append((B1[p + 3] + total - DIAG1[p] * v)[near])
+        return (B1[p + 3] + total - DIAG1[p] * v)[near]
+
+    residual = {}
+    arrived(b1_copies[4:6])
+    unpack1(1, B1, 0, 8, -3)
+    first1(range(8))
+    for p in range(1, 7):
+        second1(p, (near, far))
+    for p in range(2, 6):
+        residual[p] = residual1(p)
+    arrived(b1_copies[0:4] + b1_copies[6:8])
+    unpack1(1, B1, -3, 0, -3)
+    unpack1(1, B1, 8, 11, -3)
+    first1((-3, -2, -1, 8, 9, 10))
+    for p, rows in ((-1, (near,)), (0, (near, far)), (7, (near, far)), (8, (near,))):
+        second1(p, rows)
+    for p in (0, 1, 6, 7):
+        residual[p] = residual1(p)
 
     GB[2, gy] = 0.5 * down1(lambda p: residual[p])
     b2_copies = [post(GB.at[2, gy], GB.at[2 - d, gy], {"gx": d, "gy": e})

time: 39.2 us -> 39.2 us (level)
  no operation moved by 1% of the time
where the time goes in v7:
time: 39.2 us; the launch traced here: 39 us
  Pallas kernels  38.3 us (98%)
  local copies, waits for them, and re-layouts  0.66 us (2%)
    pallas_call x1, Pallas kernels, shards(): pl.pallas_call(kernel, out_shape=pltpu.VMEM((16, 8, 256), f32), in_specs=...  38.3 us

profile of v7, /device:TPU:1, one launch (start us, length us, event | category | flops | bytes accessed | tf_op | source)
XLA Modules:
  0.0 39.0 jit_solution(3174606208699684824)
XLA Ops:
  0.0 38.3 %vcycle.1 = f32[16,8,256]{2,1,0:T(8,128)S(1)} custom-call(f32[16,8,256]{2,1,0:T(8,128)} %src_in.1, s32[16,8,256]{2,1,0:T(8,128)} %mask_in.1, f32[16,8,256]{2,1,0:T(8,128)} %fac_in.1), custom_call_target="tpu_custom_call" | custom-call | tf_op jit(solution)/shard_map/vcycle/pallas_call | solution.py:548
  38.3 0.7 %copy.5 = f32[16,8,256]{2,1,0:T(8,128)} copy(f32[16,8,256]{2,1,0:T(8,128)S(1)} %vcycle.1) | data formatting | bytes 262144

commit v8 on v7

--- a/solution.py
+++ b/solution.py
@@ -466,8 +466,9 @@
         residual[p] = residual1(p)
 
     GB[2, gy] = 0.5 * down1(lambda p: residual[p])
+    order = [(d, e) for e in (2, 1, 3, 0) for d in (2, -2, 1, -1, 0) if d or e]
     b2_copies = [post(GB.at[2, gy], GB.at[2 - d, gy], {"gx": d, "gy": e})
-                 for e in (2, 1, 3, 0) for d in (2, -2, 1, -1, 0) if d or e]
+                 for d, e in order]
     @pl.when(gx >= 0)
     def _():
         second1(-2, (near,))
@@ -488,11 +489,12 @@
             out[c:c + CHUNK] = v[:, :, own]
     late = {id(copy) for copy in to_below + to_above}
     left([copy for copy in copies if id(copy) not in late])
-    arrived(b2_copies)
-    planes = []
-    for d in (-2, -1, 0, 1, 2):
-        planes += [jnp.where(exists("gx", d), t, 0.0) if d else t for t in rows_of([GB[2 + d, q] for q in range(4)])]
-    start = inv2 * jnp.stack(planes)
+    parts = {}
+    for d in (0, 1, -1, 2, -2):
+        arrived([copy for copy, way in zip(b2_copies, order) if way[0] == -d])
+        planes = [jnp.where(exists("gx", d), t, 0.0) if d else t for t in rows_of([GB[2 + d, q] for q in range(4)])]
+        parts[d] = inv2[4 * d + 8:4 * d + 12] * jnp.stack(planes)
+    start = jnp.concatenate([parts[d] for d in (-2, -1, 0, 1, 2)], axis=0)
     v = start
     for k in range(1, COARSE_SWEEPS):
         z = 20 - k

time: 39.2 us -> 39.1 us (level)
  no operation moved by 1% of the time
where the time goes in v8:
time: 39.1 us; the launch traced here: 39 us
  Pallas kernels  38.3 us (98%)
  local copies, waits for them, and re-layouts  0.66 us (2%)
    pallas_call x1, Pallas kernels, shards(): pl.pallas_call(kernel, out_shape=pltpu.VMEM((16, 8, 256), f32), in_specs=...  38.3 us

profile of v8, /device:TPU:1, one launch (start us, length us, event | category | flops | bytes accessed | tf_op | source)
XLA Modules:
  0.0 39.0 jit_solution(2389976848059210266)
XLA Ops:
  0.0 38.3 %vcycle.1 = f32[16,8,256]{2,1,0:T(8,128)S(1)} custom-call(f32[16,8,256]{2,1,0:T(8,128)} %src_in.1, s32[16,8,256]{2,1,0:T(8,128)} %mask_in.1, f32[16,8,256]{2,1,0:T(8,128)} %fac_in.1), custom_call_target="tpu_custom_call" | custom-call | tf_op jit(solution)/shard_map/vcycle/pallas_call | solution.py:550
  38.3 0.7 %copy.5 = f32[16,8,256]{2,1,0:T(8,128)} copy(f32[16,8,256]{2,1,0:T(8,128)S(1)} %vcycle.1) | data formatting | bytes 262144
